TPU v7x, 768 devices: a whole 4x8x12 slice. The times are simulated.
768 devices in a mesh: tiles: 192 (over y, z, core), band: 4 (over x).
Axes of the slice: x: 4, y: 8, z: 12, core: 2. Of those that a mesh axis runs over, the one named last changes fastest.
Arguments:
- optical_depth: bfloat16 [3072, 90, 4, 512], P('tiles', None, None, 'band'), may hold values from 0.00049972534 to 0.029907227
- albedo: bfloat16 [3072, 90, 512], P('tiles', None, 'band'), may hold values from 0.69921875 to 0.96875
- insolation: bfloat16 [3072, 512], P('tiles', 'band'), may hold values from 20 to 100
- sunlit: int32 [3072, 4], P('tiles', 'band'), may hold values from 0 to 1, as said below
- point_weight: float32 [4], replicated, may hold values from 0.1 to 1
- anomaly: float32 [3072, 90, 512], P('tiles', None, 'band'), may hold values from -6 to 6
Outputs:
- heating: float32 [3072, 90, 512], P('tiles', None, 'band')
- smoothed: float32 [3072, 90, 512], P('tiles', None, 'band')
Inputs may be any that keep to these rules, and one draw needn't show every extreme that they name: In every row, of two blocks that lie half of 4 sectors apart, exactly one is sunlit.
All inputs are finite; a program needn't handle non-finite values.
Results may differ from a plain program's by a relative error of at most 0.00045.
Values may be sent and summed in bfloat16 or wider, within the bound.
No kernel may reach another device: no remote copies, remote signals or barrier semaphores. Data moves between devices by JAX's collectives and lax.ppermute only.
A program may use at most 64 MiB of HBM per device.

v0:
```python
import jax
import jax.numpy as jnp
from jax import lax
from jax.sharding import PartitionSpec as P

DIFF_STEPS = 4


slant_cosine = 0.5
mixing_rate = 0.2
base_loss = 0.005


def extended(x, sides, width):
    for axis, dim in sides:
        size, length = (lax.axis_size(axis), x.shape[dim])
        up = [(i, (i + 1) % size) for i in range(size)]
        down = [(j, i) for i, j in up]
        last = lax.slice_in_dim(x, length - width, length, axis=dim)
        first = lax.slice_in_dim(x, 0, width, axis=dim)
        before = lax.ppermute(last, axis, up)
        after = lax.ppermute(first, axis, down)
        x = jnp.concatenate([before, x, after], axis=dim)
    return x


def radiate(optical_depth, albedo, sunshine, point_weight):
    levels = optical_depth.shape[1]
    depth_all = optical_depth.astype(jnp.float32)
    albedo_all = albedo.astype(jnp.float32)
    sun_float = sunshine.astype(jnp.float32)[:, None, :]
    weights = point_weight[None, :, None]
    depth_now = jnp.zeros((depth_all.shape[0], depth_all.shape[2], depth_all.shape[3]), jnp.float32)
    link_prev = jnp.zeros((depth_all.shape[0], 1, depth_all.shape[3]), jnp.float32)
    ratio_prev = depth_now
    swept_prev = depth_now
    ratio_list = []
    swept_list = []
    extinct_list = []
    for level in range(levels):
        depth_layer = depth_all[:, level]
        albedo_now = albedo_all[:, level]
        if level + 1 < levels:
            albedo_next = albedo_all[:, level + 1]
        else:
            albedo_next = jnp.zeros_like(albedo_now)
        depth_new = depth_now + depth_layer
        extinct = sun_float * (
            jnp.exp(-depth_now / slant_cosine) - jnp.exp(-depth_new / slant_cosine)
        )
        link_next = (albedo_now * albedo_next)[:, None, :]
        diagonal = (
            base_loss + 2.0 * (1.0 - albedo_now)[:, None, :] * depth_layer + link_prev + link_next
        )
        pivot = diagonal - link_prev * ratio_prev
        ratio_now = link_next / pivot
        swept_now = (albedo_now[:, None, :] * extinct + link_prev * swept_prev) / pivot
        ratio_list.append(ratio_now)
        swept_list.append(swept_now)
        extinct_list.append(extinct)
        depth_now = depth_new
        link_prev = link_next
        ratio_prev = ratio_now
        swept_prev = swept_now
    flux_next = jnp.zeros_like(depth_now)
    heat_list = [None] * levels
    for level in range(levels - 1, -1, -1):
        diffuse_flux = swept_list[level] + ratio_list[level] * flux_next
        flux_next = diffuse_flux
        absorbed = (1.0 - albedo_all[:, level])[:, None, :] * (
            extinct_list[level] + 2.0 * depth_all[:, level] * diffuse_flux
        )
        heat_list[level] = jnp.sum(absorbed * weights, axis=1)
    return jnp.stack(heat_list, axis=1)


def per_device(optical_depth, albedo, insolation, sunlit, point_weight, anomaly):
    row_count = optical_depth.shape[0]
    levels = optical_depth.shape[1]
    points = optical_depth.shape[2]
    width = optical_depth.shape[3]
    half_rows = row_count // 2
    daylit = sunlit[:, 0]
    sunshine = jnp.where(daylit[:, None] == 1, insolation, jnp.zeros_like(insolation))
    local_rank = jnp.cumsum(daylit) - daylit
    own_count = jnp.sum(daylit)
    parties = lax.axis_size("band")
    my_place = lax.axis_index("band")
    capacity = row_count // parties
    counts = lax.all_gather(own_count.reshape(1), "band", axis=0, tiled=True)
    starts = jnp.cumsum(counts) - counts
    offset = jnp.sum(jnp.where(jnp.arange(parties) < my_place, counts, 0))
    owner_band = (offset + local_rank) % parties
    slot_of_row = jnp.where(daylit == 1, owner_band * capacity + local_rank // parties, -1)
    slot_ids = jnp.arange(row_count, dtype=jnp.int32)
    matched = slot_of_row[None, :] == slot_ids[:, None]
    source_row = jnp.sum(jnp.where(matched, slot_ids[None, :], 0), axis=1)
    filled = jnp.any(matched, axis=1)
    send_depth = jnp.take(optical_depth, source_row, axis=0).reshape(
        parties, capacity, levels, points, width
    )
    send_albedo = jnp.take(albedo, source_row, axis=0).reshape(parties, capacity, levels, width)
    send_sun = jnp.where(
        filled[:, None], jnp.take(sunshine, source_row, axis=0), jnp.zeros_like(sunshine)
    )
    send_sun = send_sun.reshape(parties, capacity, width)
    got_depth, got_albedo, got_sun = (
        lax.all_to_all(send_depth, "band", split_axis=0, concat_axis=0, tiled=True),
        lax.all_to_all(send_albedo, "band", split_axis=0, concat_axis=0, tiled=True),
        lax.all_to_all(send_sun, "band", split_axis=0, concat_axis=0, tiled=True),
    )
    first_rank = (my_place - starts) % parties
    item_rank = first_rank[:, None] + parties * jnp.arange(capacity, dtype=jnp.int32)[None, :]
    item_filled = item_rank < counts[:, None]
    item_slot = jnp.where(item_filled, (starts[:, None] + item_rank) // parties, -1).reshape(
        row_count
    )
    half_ids = jnp.arange(half_rows, dtype=jnp.int32)
    chosen = item_slot[None, :] == half_ids[:, None]
    item_ids = jnp.arange(row_count, dtype=jnp.int32)
    item_of_slot = jnp.sum(jnp.where(chosen, item_ids[None, :], 0), axis=1)
    solve_depth = jnp.take(
        got_depth.reshape(row_count, levels, points, width), item_of_slot, axis=0
    )
    solve_albedo = jnp.take(got_albedo.reshape(row_count, levels, width), item_of_slot, axis=0)
    solve_sun = jnp.take(got_sun.reshape(row_count, width), item_of_slot, axis=0)
    solved = radiate(solve_depth, solve_albedo, solve_sun, point_weight)
    sent_back = jnp.take(solved, jnp.maximum(item_slot, 0), axis=0).reshape(
        parties, capacity, levels, width
    )
    returned = lax.all_to_all(sent_back, "band", split_axis=0, concat_axis=0, tiled=True).reshape(
        row_count, levels, width
    )
    picked = jnp.take(returned, jnp.maximum(slot_of_row, 0), axis=0)
    heating = jnp.where(daylit[:, None, None] == 1, picked, jnp.zeros_like(picked))
    field_now = anomaly + heating
    at_top = lax.axis_index("tiles") == 0
    at_bottom = lax.axis_index("tiles") == lax.axis_size("tiles") - 1
    for sweep in range(DIFF_STEPS):
        padded = extended(field_now, (("tiles", 0), ("band", 2)), 1)
        row_above = jnp.where(at_top, 0.0, padded[0:1, :, 1:-1])
        row_below = jnp.where(at_bottom, 0.0, padded[-1:, :, 1:-1])
        centre = padded[1:-1, :, 1:-1]
        north_south = jnp.concatenate([centre[1:], row_below], axis=0) + jnp.concatenate(
            [row_above, centre[:-1]], axis=0
        )
        east_west = padded[1:-1, :, :-2] + padded[1:-1, :, 2:]
        field_now = field_now + mixing_rate * (north_south + east_west - 4.0 * field_now)
    return (heating, field_now)


def solution(mesh):
    placed = (
        P("tiles", None, None, "band"),
        P("tiles", None, "band"),
        P("tiles", "band"),
        P("tiles", "band"),
        P(),
        P("tiles", None, "band"),
    )
    return jax.shard_map(
        per_device,
        mesh=mesh,
        in_specs=placed,
        out_specs=(P("tiles", None, "band"), P("tiles", None, "band")),
        check_vma=False,
    )
```

profile of v0, /device:TPU:2, one launch (start us, length us, event | category | flops | bytes accessed | tf_op | source)
XLA Modules:
  0.0 228.1 jit_solution(12266109133578363221)
XLA Ops:
  5.5 13.1 %all-reduce = s32[4]{0:T(128)S(1)} all-reduce(s32[4]{0:T(128)S(1)} %dynamic-update-slice), channel_id=1, replica_groups=mesh['tiles'=192,'band'=4] {'band'}, use_global_device_ids=true, to_apply=%add | all-reduce | flops 4 | bytes 32
  19.5 1.9 compare_reduce_fusion
  24.7 7.1 %all-to-all-start.1 = ((bf16[4,4,128]{2,1,0:T(4,128)(2,1)}), bf16[4,4,128]{2,1,0:T(4,128)(2,1)S(1)}, u32[]{:S(2)}, u32[]{:S(2)}) async-start(bf16[4,4,128]{2,1,0:T(4,128)(2,1)} %select_select_fusion.1), calls=%async_computation.1 | async-start | bytes 8192 | tf_op jit(solution)/shard_map/all_to_all | solution.py:110
  33.0 2.6 %gather_fusion = bf16[16,90,128]{2,0,1:T(8,128)(2,1)S(1)} fusion(bf16[16,90,128]{2,0,1:T(8,128)(2,1)} %param.7, s32[1024]{0:T(1024)S(1)} %pad_clamp_fusion.3), kind=kCustom, calls=%fused_computation | custom fusion | bytes 737344 | tf_op jit(solution)/shard_map/jit(_take)/gather | solution.py:102
  36.6 1.8 gather_fusion.4
  38.4 1.9 broadcast_select_fusion
  40.4 4.8 %all-to-all-start = ((bf16[4,4,90,128]{3,1,2,0:T(4,128)(2,1)}), bf16[4,4,90,128]{3,1,2,0:T(4,128)(2,1)S(1)}, u32[]{:S(2)}, u32[]{:S(2)}) async-start(bf16[4,4,90,128]{3,1,2,0:T(4,128)(2,1)} %copy_select_fusion.2), calls=%async_computation | async-start | bytes 737280 | tf_op jit(solution)/shard_map/all_to_all | solution.py:109
  46.4 6.5 %all-to-all-done = bf16[4,4,90,128]{3,1,2,0:T(4,128)(2,1)S(1)} async-done(((bf16[4,4,90,128]{3,1,2,0:T(4,128)(2,1)}), bf16[4,4,90,128]{3,1,2,0:T(4,128)(2,1)S(1)}, u32[]{:S(2)}, u32[]{:S(2)}) %all-to-all-start) | async-done | bytes 368672 | tf_op jit(solution)/shard_map/all_to_all | solution.py:109
  52.9 5.0 %all-to-all-start.2 = ((bf16[4,4,90,4,128]{4,3,2,1,0:T(4,128)(2,1)}), bf16[4,4,90,4,128]{4,3,2,1,0:T(4,128)(2,1)S(1)}, u32[]{:S(2)}, u32[]{:S(2)}) async-start(bf16[4,4,90,4,128]{4,3,2,1,0:T(4,128)(2,1)} %broadcast_select_fusion), calls=%async_computation.2 | async-start | bytes 2949120 | tf_op jit(solution)/shard_map/all_to_all | solution.py:108
  58.7 1.6 gather_fusion.1
  76.1 2.1 gather_fusion.5
  80.6 2.1 add_divide_fusion.43
  83.1 4.0 %add_divide_fusion = (f32[8,4,128]{2,0,1:T(8,128)S(1)}, f32[8,4,128]{2,0,1:T(8,128)S(1)}, f32[8,4,128]{2,0,1:T(8,128)S(1)}, f32[8,4,128]{2,0,1:T(8,128)S(1)}, f3...) fusion(f32[8,128]{1,0:T(8,128)} %bitcast.2316, ...), kind=kLoop, calls=%fused_computation.348 | loop fusion | flops 2801664 | bytes 3416064 | tf_op jit(solution)/shard_map/div | solution.py:57
  96.6 4.8 %all-to-all-start.3 = ((f32[4,4,90,128]{3,1,2,0:T(4,128)}), f32[4,4,90,128]{3,1,2,0:T(4,128)S(1)}, u32[]{:S(2)}, u32[]{:S(2)}) async-start(f32[4,4,90,128]{3,1,2,0:T(4,128)} %copy_select_fusion), calls=%async_computation.3 | async-start | bytes 1474560 | tf_op jit(solution)/shard_map/all_to_all | solution.py:131
  101.6 7.6 %all-to-all-done.3 = f32[4,4,90,128]{3,1,2,0:T(4,128)S(1)} async-done(((f32[4,4,90,128]{3,1,2,0:T(4,128)}), f32[4,4,90,128]{3,1,2,0:T(4,128)S(1)}, u32[]{:S(2)}, u32[]{:S(2)}) %all-to-all-start.3) | async-done | bytes 737312 | tf_op jit(solution)/shard_map/all_to_all | solution.py:131
  110.7 1.8 copy_add_fusion
  112.6 1.9 collective-permute-start.1
  114.5 7.0 %collective-permute-start = (f32[1,90,128]{2,1,0:T(8,128)S(1)}, f32[1,90,128]{2,1,0:T(8,128)S(1)}, u32[]{:S(2)}, u32[]{:S(2)}) collective-permute-start(f32[1,90,128]{2,1,0:T(8,128)S(1)} %get-tuple-element.478), channel_id=1, source_target_pairs={{4,0},{8,4},{12,8},{16,12},{20,16},{24,20},{28,24},{32,28},{36,32}... | collective-permute-start | bytes 138248 | tf_op jit(solution)/shard_map/ppermute | solution.py:22
  124.1 1.5 fusion.188
  125.6 1.5 copy.509
  127.1 1.5 copy.511
  128.6 3.4 %collective-permute-start.3 = (f32[18,90,1]{1,2,0:T(1,128)S(1)}, f32[18,90,1]{1,2,0:T(1,128)S(1)}, u32[]{:S(2)}, u32[]{:S(2)}) collective-permute-start(f32[18,90,1]{1,2,0:T(1,128)S(1)} %copy.511), channel_id=1, source_target_pairs={{1,0},{2,1},{3,2},{0,3},{5,4},{6,5},{7,6},{4,7},{9,8},{10,9},{11,1... | collective-permute-start | bytes 19448 | tf_op jit(solution)/shard_map/ppermute | solution.py:22
  132.0 2.7 %collective-permute-start.2 = (f32[18,90,1]{1,2,0:T(1,128)S(1)}, f32[18,90,1]{1,2,0:T(1,128)S(1)}, u32[]{:S(2)}, u32[]{:S(2)}) collective-permute-start(f32[18,90,1]{1,2,0:T(1,128)S(1)} %copy.509), channel_id=1, source_target_pairs={{0,1},{1,2},{2,3},{3,0},{4,5},{5,6},{6,7},{7,4},{8,9},{9,10},{10,1... | collective-permute-start | bytes 19448 | tf_op jit(solution)/shard_map/ppermute | solution.py:21
  134.7 2.8 %collective-permute-done.2 = f32[18,90,1]{1,2,0:T(1,128)S(1)} collective-permute-done((f32[18,90,1]{1,2,0:T(1,128)S(1)}, f32[18,90,1]{1,2,0:T(1,128)S(1)}, u32[]{:S(2)}, u32[]{:S(2)}) %collective-permute-start.2) | collective-permute-done | bytes 6512 | tf_op jit(solution)/shard_map/ppermute | solution.py:21
  140.1 2.5 %fusion.19 = f32[16,90,128]{2,1,0:T(8,128)S(1)} fusion(f32[16,90,128]{2,1,0:T(8,128)S(1)} %get-tuple-element.102, f32[18,90,1]{2,1,0:T(8,128)} %copy.512, f32[1,90,128]{2,1,0:T(8,128)S(1)} %collective-permute-done, f32[1,90,128]{2,1,0:T(8,128)S(1)} %collective-permute-done.1, f32[18,90,1]{2,1,0:T(8,128)} %copy.510, ...), kind=kLoop, calls=%fused_computation.51 | loop fusion | flops 2764800 | bytes 3054240 | tf_op jit(solution)/shard_map/add | solution.py:148
  142.6 1.9 collective-permute-start.5
  144.6 7.0 %collective-permute-start.4 = (f32[1,90,128]{2,1,0:T(8,128)S(1)}, f32[1,90,128]{2,1,0:T(8,128)S(1)}, u32[]{:S(2)}, u32[]{:S(2)}) collective-permute-start(f32[1,90,128]{2,1,0:T(8,128)S(1)} %get-tuple-element.474), channel_id=1, source_target_pairs={{4,0},{8,4},{12,8},{16,12},{20,16},{24,20},{28,24},{32,28},{36,32}... | collective-permute-start | bytes 138248 | tf_op jit(solution)/shard_map/ppermute | solution.py:22
  154.6 1.5 copy.513
  156.4 4.3 %collective-permute-start.7 = (f32[18,90,1]{1,2,0:T(1,128)S(1)}, f32[18,90,1]{1,2,0:T(1,128)S(1)}, u32[]{:S(2)}, u32[]{:S(2)}) collective-permute-start(f32[18,90,1]{1,2,0:T(1,128)S(1)} %copy.515), channel_id=1, source_target_pairs={{1,0},{2,1},{3,2},{0,3},{5,4},{6,5},{7,6},{4,7},{9,8},{10,9},{11,1... | collective-permute-start | bytes 19448 | tf_op jit(solution)/shard_map/ppermute | solution.py:22
  160.7 1.9 collective-permute-start.6
  162.6 3.6 %collective-permute-done.6 = f32[18,90,1]{1,2,0:T(1,128)S(1)} collective-permute-done((f32[18,90,1]{1,2,0:T(1,128)S(1)}, f32[18,90,1]{1,2,0:T(1,128)S(1)}, u32[]{:S(2)}, u32[]{:S(2)}) %collective-permute-start.6) | collective-permute-done | bytes 6512 | tf_op jit(solution)/shard_map/ppermute | solution.py:21
  168.9 2.5 %fusion.14 = f32[16,90,128]{2,1,0:T(8,128)S(1)} fusion(f32[16,90,128]{2,1,0:T(8,128)S(1)} %fusion.19, f32[18,90,1]{2,1,0:T(8,128)} %copy.516, f32[1,90,128]{2,1,0:T(8,128)S(1)} %collective-permute-done.4, f32[1,90,128]{2,1,0:T(8,128)S(1)} %collective-permute-done.5, f32[18,90,1]{2,1,0:T(8,128)} %copy.514, f32[1,90,128]{2,1,0:T(8,128)S(1)} %broadcast_select_fusion.6, ...), kind=kLoop, calls=%fused_computation.40 | loop fusion | flops 2764800 | bytes 3054240 | tf_op jit(solution)/shard_map/add | solution.py:148
  171.4 1.9 collective-permute-start.9
  173.3 7.0 %collective-permute-start.8 = (f32[1,90,128]{2,1,0:T(8,128)S(1)}, f32[1,90,128]{2,1,0:T(8,128)S(1)}, u32[]{:S(2)}, u32[]{:S(2)}) collective-permute-start(f32[1,90,128]{2,1,0:T(8,128)S(1)} %get-tuple-element.470), channel_id=1, source_target_pairs={{4,0},{8,4},{12,8},{16,12},{20,16},{24,20},{28,24},{32,28},{36,32}... | collective-permute-start | bytes 138248 | tf_op jit(solution)/shard_map/ppermute | solution.py:22
  182.1 1.5 fusion.186
  183.6 1.5 copy.517
  185.0 1.5 copy.519
  186.5 3.1 %collective-permute-start.11 = (f32[18,90,1]{1,2,0:T(1,128)S(1)}, f32[18,90,1]{1,2,0:T(1,128)S(1)}, u32[]{:S(2)}, u32[]{:S(2)}) collective-permute-start(f32[18,90,1]{1,2,0:T(1,128)S(1)} %copy.519), channel_id=1, source_target_pairs={{1,0},{2,1},{3,2},{0,3},{5,4},{6,5},{7,6},{4,7},{9,8},{10,9},{11,1... | collective-permute-start | bytes 19448 | tf_op jit(solution)/shard_map/ppermute | solution.py:22
  189.7 2.7 %collective-permute-start.10 = (f32[18,90,1]{1,2,0:T(1,128)S(1)}, f32[18,90,1]{1,2,0:T(1,128)S(1)}, u32[]{:S(2)}, u32[]{:S(2)}) collective-permute-start(f32[18,90,1]{1,2,0:T(1,128)S(1)} %copy.517), channel_id=1, source_target_pairs={{0,1},{1,2},{2,3},{3,0},{4,5},{5,6},{6,7},{7,4},{8,9},{9,10},{10,1... | collective-permute-start | bytes 19448 | tf_op jit(solution)/shard_map/ppermute | solution.py:21
  192.4 2.8 %collective-permute-done.10 = f32[18,90,1]{1,2,0:T(1,128)S(1)} collective-permute-done((f32[18,90,1]{1,2,0:T(1,128)S(1)}, f32[18,90,1]{1,2,0:T(1,128)S(1)}, u32[]{:S(2)}, u32[]{:S(2)}) %collective-permute-start.10) | collective-permute-done | bytes 6512 | tf_op jit(solution)/shard_map/ppermute | solution.py:21
  197.9 2.5 %fusion.9 = f32[16,90,128]{2,1,0:T(8,128)S(1)} fusion(f32[16,90,128]{2,1,0:T(8,128)S(1)} %fusion.14, f32[18,90,1]{2,1,0:T(8,128)} %copy.520, f32[1,90,128]{2,1,0:T(8,128)S(1)} %collective-permute-done.8, f32[1,90,128]{2,1,0:T(8,128)S(1)} %collective-permute-done.9, f32[18,90,1]{2,1,0:T(8,128)} %copy.518, f32[1,90,128]{2,1,0:T(8,128)S(1)} %broadcast_select_fusion.4, ...), kind=kLoop, calls=%fused_computation.29 | loop fusion | flops 2764800 | bytes 3054240 | tf_op jit(solution)/shard_map/add | solution.py:148
  200.4 1.9 collective-permute-start.13
  202.3 7.0 %collective-permute-start.12 = (f32[1,90,128]{2,1,0:T(8,128)S(1)}, f32[1,90,128]{2,1,0:T(8,128)S(1)}, u32[]{:S(2)}, u32[]{:S(2)}) collective-permute-start(f32[1,90,128]{2,1,0:T(8,128)S(1)} %get-tuple-element.466), channel_id=1, source_target_pairs={{4,0},{8,4},{12,8},{16,12},{20,16},{24,20},{28,24},{32,28},{36,32}... | collective-permute-start | bytes 138248 | tf_op jit(solution)/shard_map/ppermute | solution.py:22
  212.3 1.5 copy.521
  214.1 3.1 %collective-permute-start.15 = (f32[18,90,1]{1,2,0:T(1,128)S(1)}, f32[18,90,1]{1,2,0:T(1,128)S(1)}, u32[]{:S(2)}, u32[]{:S(2)}) collective-permute-start(f32[18,90,1]{1,2,0:T(1,128)S(1)} %copy.523), channel_id=1, source_target_pairs={{1,0},{2,1},{3,2},{0,3},{5,4},{6,5},{7,6},{4,7},{9,8},{10,9},{11,1... | collective-permute-start | bytes 19448 | tf_op jit(solution)/shard_map/ppermute | solution.py:22
  217.2 2.7 %collective-permute-start.14 = (f32[18,90,1]{1,2,0:T(1,128)S(1)}, f32[18,90,1]{1,2,0:T(1,128)S(1)}, u32[]{:S(2)}, u32[]{:S(2)}) collective-permute-start(f32[18,90,1]{1,2,0:T(1,128)S(1)} %copy.521), channel_id=1, source_target_pairs={{0,1},{1,2},{2,3},{3,0},{4,5},{5,6},{6,7},{7,4},{8,9},{9,10},{10,1... | collective-permute-start | bytes 19448 | tf_op jit(solution)/shard_map/ppermute | solution.py:21
  220.0 2.8 %collective-permute-done.14 = f32[18,90,1]{1,2,0:T(1,128)S(1)} collective-permute-done((f32[18,90,1]{1,2,0:T(1,128)S(1)}, f32[18,90,1]{1,2,0:T(1,128)S(1)}, u32[]{:S(2)}, u32[]{:S(2)}) %collective-permute-start.14) | collective-permute-done | bytes 6512 | tf_op jit(solution)/shard_map/ppermute | solution.py:21
  224.5 2.3 fusion.4
  (426 shorter events, 63.3 us)
Async XLA Ops:
  0.6 35.9 %copy-start = (bf16[16,90,4,128]{3,2,1,0:T(4,128)(2,1)S(1)}, bf16[16,90,4,128]{3,2,1,0:T(4,128)(2,1)}, u32[]{:S(2)}) copy-start(bf16[16,90,4,128]{3,2,1,0:T(4,128)(2,1)} %param.6) | copy-start | bytes 4423684
  21.4 11.5 %copy-start.128 = (pred[16]{0:T(512)(128)(4,1)}, pred[16]{0:T(512)(128)(4,1)S(1)}, u32[]{:S(2)}) copy-start(pred[16]{0:T(512)(128)(4,1)S(1)} %get-tuple-element.839) | copy-start | bytes 52
  24.7 15.6 %all-to-all-start.1 = ((bf16[4,4,128]{2,1,0:T(4,128)(2,1)}), bf16[4,4,128]{2,1,0:T(4,128)(2,1)S(1)}, u32[]{:S(2)}, u32[]{:S(2)}) async-start(bf16[4,4,128]{2,1,0:T(4,128)(2,1)} %select_select_fusion.1), calls=%async_computation.1 | async-start | bytes 8192 | tf_op jit(solution)/shard_map/all_to_all | solution.py:110
  32.8 27.6 %copy-start.131 = (pred[8]{0:T(512)(128)(4,1)}, pred[8]{0:T(512)(128)(4,1)S(1)}, u32[]{:S(2)}) copy-start(pred[8]{0:T(512)(128)(4,1)S(1)} %compare_and_fusion.1) | copy-start | bytes 28
  40.4 18.4 %copy-start.130 = (s32[1024]{0:T(1024)}, s32[1024]{0:T(1024)S(1)}, u32[]{:S(2)}) copy-start(s32[1024]{0:T(1024)S(1)} %pad_clamp_fusion.2) | copy-start | bytes 12292
  40.4 12.6 %all-to-all-start = ((bf16[4,4,90,128]{3,1,2,0:T(4,128)(2,1)}), bf16[4,4,90,128]{3,1,2,0:T(4,128)(2,1)S(1)}, u32[]{:S(2)}, u32[]{:S(2)}) async-start(bf16[4,4,90,128]{3,1,2,0:T(4,128)(2,1)} %copy_select_fusion.2), calls=%async_computation | async-start | bytes 737280 | tf_op jit(solution)/shard_map/all_to_all | solution.py:109
  52.9 23.2 %all-to-all-start.2 = ((bf16[4,4,90,4,128]{4,3,2,1,0:T(4,128)(2,1)}), bf16[4,4,90,4,128]{4,3,2,1,0:T(4,128)(2,1)S(1)}, u32[]{:S(2)}, u32[]{:S(2)}) async-start(bf16[4,4,90,4,128]{4,3,2,1,0:T(4,128)(2,1)} %broadcast_select_fusion), calls=%async_computation.2 | async-start | bytes 2949120 | tf_op jit(solution)/shard_map/all_to_all | solution.py:108
  66.9 11.4 %copy-start.132 = (pred[8]{0:T(512)(128)(4,1)S(1)}, pred[8]{0:T(512)(128)(4,1)}, u32[]{:S(2)}) copy-start(pred[8]{0:T(512)(128)(4,1)} %copy-done.131) | copy-start | bytes 28
  83.1 5.1 %copy-start.1 = (f32[4]{0:T(128)S(1)}, f32[4]{0:T(128)}, u32[]{:S(2)}) copy-start(f32[4]{0:T(128)} %param.10) | copy-start | bytes 52
  83.1 5.1 %copy-start.63 = (f32[8,1,128]{2,1,0:T(1,128)S(1)}, f32[8,1,128]{2,1,0:T(1,128)}, u32[]{:S(2)}) copy-start(f32[8,1,128]{2,1,0:T(1,128)} %get-tuple-element.719) | copy-start | bytes 12292
  83.1 5.1 %copy-start.64 = (f32[8,1,128]{2,1,0:T(1,128)S(1)}, f32[8,1,128]{2,1,0:T(1,128)}, u32[]{:S(2)}) copy-start(f32[8,1,128]{2,1,0:T(1,128)} %get-tuple-element.725) | copy-start | bytes 12292
  83.1 5.9 %copy-start.58 = (f32[8,1,128]{2,1,0:T(1,128)S(1)}, f32[8,1,128]{2,1,0:T(1,128)}, u32[]{:S(2)}) copy-start(f32[8,1,128]{2,1,0:T(1,128)} %get-tuple-element.710) | copy-start | bytes 12292
  83.1 5.9 %copy-start.61 = (f32[8,1,128]{2,1,0:T(1,128)S(1)}, f32[8,1,128]{2,1,0:T(1,128)}, u32[]{:S(2)}) copy-start(f32[8,1,128]{2,1,0:T(1,128)} %get-tuple-element.716) | copy-start | bytes 12292
  83.1 5.9 %copy-start.62 = (f32[8,1,128]{2,1,0:T(1,128)S(1)}, f32[8,1,128]{2,1,0:T(1,128)}, u32[]{:S(2)}) copy-start(f32[8,1,128]{2,1,0:T(1,128)} %get-tuple-element.722) | copy-start | bytes 12292
  87.2 2.7 %copy-start.53 = (f32[8,1,128]{2,1,0:T(1,128)S(1)}, f32[8,1,128]{2,1,0:T(1,128)}, u32[]{:S(2)}) copy-start(f32[8,1,128]{2,1,0:T(1,128)} %get-tuple-element.698) | copy-start | bytes 12292
  87.2 2.7 %copy-start.54 = (f32[8,1,128]{2,1,0:T(1,128)S(1)}, f32[8,1,128]{2,1,0:T(1,128)}, u32[]{:S(2)}) copy-start(f32[8,1,128]{2,1,0:T(1,128)} %get-tuple-element.707) | copy-start | bytes 12292
  87.2 2.9 %copy-start.52 = (f32[8,1,128]{2,1,0:T(1,128)S(1)}, f32[8,1,128]{2,1,0:T(1,128)}, u32[]{:S(2)}) copy-start(f32[8,1,128]{2,1,0:T(1,128)} %get-tuple-element.704) | copy-start | bytes 12292
  87.2 3.0 %copy-start.59 = (f32[8,1,128]{2,1,0:T(1,128)S(1)}, f32[8,1,128]{2,1,0:T(1,128)}, u32[]{:S(2)}) copy-start(f32[8,1,128]{2,1,0:T(1,128)} %get-tuple-element.672) | copy-start | bytes 12292
  87.2 3.0 %copy-start.60 = (f32[8,1,128]{2,1,0:T(1,128)S(1)}, f32[8,1,128]{2,1,0:T(1,128)}, u32[]{:S(2)}) copy-start(f32[8,1,128]{2,1,0:T(1,128)} %get-tuple-element.677) | copy-start | bytes 12292
  87.2 2.8 %copy-start.120 = (f32[8,1,128]{2,1,0:T(1,128)S(1)}, f32[8,1,128]{2,1,0:T(1,128)}, u32[]{:S(2)}) copy-start(f32[8,1,128]{2,1,0:T(1,128)} %get-tuple-element.686) | copy-start | bytes 12292
  87.2 2.8 %copy-start.121 = (f32[8,1,128]{2,1,0:T(1,128)S(1)}, f32[8,1,128]{2,1,0:T(1,128)}, u32[]{:S(2)}) copy-start(f32[8,1,128]{2,1,0:T(1,128)} %get-tuple-element.692) | copy-start | bytes 12292
  87.2 2.8 %copy-start.122 = (f32[8,1,128]{2,1,0:T(1,128)S(1)}, f32[8,1,128]{2,1,0:T(1,128)}, u32[]{:S(2)}) copy-start(f32[8,1,128]{2,1,0:T(1,128)} %get-tuple-element.697) | copy-start | bytes 12292
  87.3 3.0 %copy-start.118 = (f32[8,1,128]{2,1,0:T(1,128)S(1)}, f32[8,1,128]{2,1,0:T(1,128)}, u32[]{:S(2)}) copy-start(f32[8,1,128]{2,1,0:T(1,128)} %get-tuple-element.683) | copy-start | bytes 12292
  87.3 3.0 %copy-start.119 = (f32[8,1,128]{2,1,0:T(1,128)S(1)}, f32[8,1,128]{2,1,0:T(1,128)}, u32[]{:S(2)}) copy-start(f32[8,1,128]{2,1,0:T(1,128)} %get-tuple-element.689) | copy-start | bytes 12292
  87.3 3.1 %copy-start.50 = (f32[8,1,128]{2,1,0:T(1,128)S(1)}, f32[8,1,128]{2,1,0:T(1,128)}, u32[]{:S(2)}) copy-start(f32[8,1,128]{2,1,0:T(1,128)} %get-tuple-element.662) | copy-start | bytes 12292
  87.3 3.1 %copy-start.51 = (f32[8,1,128]{2,1,0:T(1,128)S(1)}, f32[8,1,128]{2,1,0:T(1,128)}, u32[]{:S(2)}) copy-start(f32[8,1,128]{2,1,0:T(1,128)} %get-tuple-element.668) | copy-start | bytes 12292
  87.3 3.1 %copy-start.55 = (f32[8,1,128]{2,1,0:T(1,128)S(1)}, f32[8,1,128]{2,1,0:T(1,128)}, u32[]{:S(2)}) copy-start(f32[8,1,128]{2,1,0:T(1,128)} %get-tuple-element.669) | copy-start | bytes 12292
  87.3 3.1 %copy-start.56 = (f32[8,1,128]{2,1,0:T(1,128)S(1)}, f32[8,1,128]{2,1,0:T(1,128)}, u32[]{:S(2)}) copy-start(f32[8,1,128]{2,1,0:T(1,128)} %get-tuple-element.680) | copy-start | bytes 12292
  95.2 6.2 %copy-start.11 = (s32[16,1]{1,0:T(8,128)S(1)}, s32[16,1]{1,0:T(8,128)}, u32[]{:S(2)}) copy-start(s32[16,1]{1,0:T(8,128)} %get-tuple-element.105) | copy-start | bytes 196
  96.6 12.6 %all-to-all-start.3 = ((f32[4,4,90,128]{3,1,2,0:T(4,128)}), f32[4,4,90,128]{3,1,2,0:T(4,128)S(1)}, u32[]{:S(2)}, u32[]{:S(2)}) async-start(f32[4,4,90,128]{3,1,2,0:T(4,128)} %copy_select_fusion), calls=%async_computation.3 | async-start | bytes 1474560 | tf_op jit(solution)/shard_map/all_to_all | solution.py:131
  101.5 9.2 %copy-start.129 = (pred[16]{0:T(512)(128)(4,1)S(1)}, pred[16]{0:T(512)(128)(4,1)}, u32[]{:S(2)}) copy-start(pred[16]{0:T(512)(128)(4,1)} %copy-done.128) | copy-start | bytes 52
  101.5 9.2 %copy-start.134 = (pred[16]{0:T(512)(128)(4,1)S(1)}, pred[16]{0:T(512)(128)(4,1)}, u32[]{:S(2)}) copy-start(pred[16]{0:T(512)(128)(4,1)} %get-tuple-element.104) | copy-start | bytes 52
  112.6 11.5 %collective-permute-start.1 = (f32[1,90,128]{2,1,0:T(8,128)S(1)}, f32[1,90,128]{2,1,0:T(8,128)S(1)}, u32[]{:S(2)}, u32[]{:S(2)}) collective-permute-start(f32[1,90,128]{2,1,0:T(8,128)S(1)} %get-tuple-element.477), channel_id=1, source_target_pairs={{0,4},{4,8},{8,12},{12,16},{16,20},{20,24},{24,28},{28,32},{32,36}... | collective-permute-start | bytes 138248 | tf_op jit(solution)/shard_map/ppermute | solution.py:21
  114.5 9.5 %collective-permute-start = (f32[1,90,128]{2,1,0:T(8,128)S(1)}, f32[1,90,128]{2,1,0:T(8,128)S(1)}, u32[]{:S(2)}, u32[]{:S(2)}) collective-permute-start(f32[1,90,128]{2,1,0:T(8,128)S(1)} %get-tuple-element.478), channel_id=1, source_target_pairs={{4,0},{8,4},{12,8},{16,12},{20,16},{24,20},{28,24},{32,28},{36,32}... | collective-permute-start | bytes 138248 | tf_op jit(solution)/shard_map/ppermute | solution.py:22
  128.6 10.3 %collective-permute-start.3 = (f32[18,90,1]{1,2,0:T(1,128)S(1)}, f32[18,90,1]{1,2,0:T(1,128)S(1)}, u32[]{:S(2)}, u32[]{:S(2)}) collective-permute-start(f32[18,90,1]{1,2,0:T(1,128)S(1)} %copy.511), channel_id=1, source_target_pairs={{1,0},{2,1},{3,2},{0,3},{5,4},{6,5},{7,6},{4,7},{9,8},{10,9},{11,1... | collective-permute-start | bytes 19448 | tf_op jit(solution)/shard_map/ppermute | solution.py:22
  132.0 5.6 %collective-permute-start.2 = (f32[18,90,1]{1,2,0:T(1,128)S(1)}, f32[18,90,1]{1,2,0:T(1,128)S(1)}, u32[]{:S(2)}, u32[]{:S(2)}) collective-permute-start(f32[18,90,1]{1,2,0:T(1,128)S(1)} %copy.509), channel_id=1, source_target_pairs={{0,1},{1,2},{2,3},{3,0},{4,5},{5,6},{6,7},{7,4},{8,9},{9,10},{10,1... | collective-permute-start | bytes 19448 | tf_op jit(solution)/shard_map/ppermute | solution.py:21
  142.6 10.2 %collective-permute-start.5 = (f32[1,90,128]{2,1,0:T(8,128)S(1)}, f32[1,90,128]{2,1,0:T(8,128)S(1)}, u32[]{:S(2)}, u32[]{:S(2)}) collective-permute-start(f32[1,90,128]{2,1,0:T(8,128)S(1)} %get-tuple-element.473), channel_id=1, source_target_pairs={{0,4},{4,8},{8,12},{12,16},{16,20},{20,24},{24,28},{28,32},{32,36}... | collective-permute-start | bytes 138248 | tf_op jit(solution)/shard_map/ppermute | solution.py:21
  144.6 8.7 %collective-permute-start.4 = (f32[1,90,128]{2,1,0:T(8,128)S(1)}, f32[1,90,128]{2,1,0:T(8,128)S(1)}, u32[]{:S(2)}, u32[]{:S(2)}) collective-permute-start(f32[1,90,128]{2,1,0:T(8,128)S(1)} %get-tuple-element.474), channel_id=1, source_target_pairs={{4,0},{8,4},{12,8},{16,12},{20,16},{24,20},{28,24},{32,28},{36,32}... | collective-permute-start | bytes 138248 | tf_op jit(solution)/shard_map/ppermute | solution.py:22
  156.4 11.2 %collective-permute-start.7 = (f32[18,90,1]{1,2,0:T(1,128)S(1)}, f32[18,90,1]{1,2,0:T(1,128)S(1)}, u32[]{:S(2)}, u32[]{:S(2)}) collective-permute-start(f32[18,90,1]{1,2,0:T(1,128)S(1)} %copy.515), channel_id=1, source_target_pairs={{1,0},{2,1},{3,2},{0,3},{5,4},{6,5},{7,6},{4,7},{9,8},{10,9},{11,1... | collective-permute-start | bytes 19448 | tf_op jit(solution)/shard_map/ppermute | solution.py:22
  160.7 5.6 %collective-permute-start.6 = (f32[18,90,1]{1,2,0:T(1,128)S(1)}, f32[18,90,1]{1,2,0:T(1,128)S(1)}, u32[]{:S(2)}, u32[]{:S(2)}) collective-permute-start(f32[18,90,1]{1,2,0:T(1,128)S(1)} %copy.513), channel_id=1, source_target_pairs={{0,1},{1,2},{2,3},{3,0},{4,5},{5,6},{6,7},{7,4},{8,9},{9,10},{10,1... | collective-permute-start | bytes 19448 | tf_op jit(solution)/shard_map/ppermute | solution.py:21
  171.4 10.2 %collective-permute-start.9 = (f32[1,90,128]{2,1,0:T(8,128)S(1)}, f32[1,90,128]{2,1,0:T(8,128)S(1)}, u32[]{:S(2)}, u32[]{:S(2)}) collective-permute-start(f32[1,90,128]{2,1,0:T(8,128)S(1)} %get-tuple-element.469), channel_id=1, source_target_pairs={{0,4},{4,8},{8,12},{12,16},{16,20},{20,24},{24,28},{28,32},{32,36}... | collective-permute-start | bytes 138248 | tf_op jit(solution)/shard_map/ppermute | solution.py:21
  173.3 8.7 %collective-permute-start.8 = (f32[1,90,128]{2,1,0:T(8,128)S(1)}, f32[1,90,128]{2,1,0:T(8,128)S(1)}, u32[]{:S(2)}, u32[]{:S(2)}) collective-permute-start(f32[1,90,128]{2,1,0:T(8,128)S(1)} %get-tuple-element.470), channel_id=1, source_target_pairs={{4,0},{8,4},{12,8},{16,12},{20,16},{24,20},{28,24},{32,28},{36,32}... | collective-permute-start | bytes 138248 | tf_op jit(solution)/shard_map/ppermute | solution.py:22
  186.5 10.0 %collective-permute-start.11 = (f32[18,90,1]{1,2,0:T(1,128)S(1)}, f32[18,90,1]{1,2,0:T(1,128)S(1)}, u32[]{:S(2)}, u32[]{:S(2)}) collective-permute-start(f32[18,90,1]{1,2,0:T(1,128)S(1)} %copy.519), channel_id=1, source_target_pairs={{1,0},{2,1},{3,2},{0,3},{5,4},{6,5},{7,6},{4,7},{9,8},{10,9},{11,1... | collective-permute-start | bytes 19448 | tf_op jit(solution)/shard_map/ppermute | solution.py:22
  189.7 5.6 %collective-permute-start.10 = (f32[18,90,1]{1,2,0:T(1,128)S(1)}, f32[18,90,1]{1,2,0:T(1,128)S(1)}, u32[]{:S(2)}, u32[]{:S(2)}) collective-permute-start(f32[18,90,1]{1,2,0:T(1,128)S(1)} %copy.517), channel_id=1, source_target_pairs={{0,1},{1,2},{2,3},{3,0},{4,5},{5,6},{6,7},{7,4},{8,9},{9,10},{10,1... | collective-permute-start | bytes 19448 | tf_op jit(solution)/shard_map/ppermute | solution.py:21
  200.4 10.2 %collective-permute-start.13 = (f32[1,90,128]{2,1,0:T(8,128)S(1)}, f32[1,90,128]{2,1,0:T(8,128)S(1)}, u32[]{:S(2)}, u32[]{:S(2)}) collective-permute-start(f32[1,90,128]{2,1,0:T(8,128)S(1)} %get-tuple-element.465), channel_id=1, source_target_pairs={{0,4},{4,8},{8,12},{12,16},{16,20},{20,24},{24,28},{28,32},{32,36}... | collective-permute-start | bytes 138248 | tf_op jit(solution)/shard_map/ppermute | solution.py:21
  202.3 8.7 %collective-permute-start.12 = (f32[1,90,128]{2,1,0:T(8,128)S(1)}, f32[1,90,128]{2,1,0:T(8,128)S(1)}, u32[]{:S(2)}, u32[]{:S(2)}) collective-permute-start(f32[1,90,128]{2,1,0:T(8,128)S(1)} %get-tuple-element.466), channel_id=1, source_target_pairs={{4,0},{8,4},{12,8},{16,12},{20,16},{24,20},{28,24},{32,28},{36,32}... | collective-permute-start | bytes 138248 | tf_op jit(solution)/shard_map/ppermute | solution.py:22
  214.1 9.1 %collective-permute-start.15 = (f32[18,90,1]{1,2,0:T(1,128)S(1)}, f32[18,90,1]{1,2,0:T(1,128)S(1)}, u32[]{:S(2)}, u32[]{:S(2)}) collective-permute-start(f32[18,90,1]{1,2,0:T(1,128)S(1)} %copy.523), channel_id=1, source_target_pairs={{1,0},{2,1},{3,2},{0,3},{5,4},{6,5},{7,6},{4,7},{9,8},{10,9},{11,1... | collective-permute-start | bytes 19448 | tf_op jit(solution)/shard_map/ppermute | solution.py:22
  217.2 5.6 %collective-permute-start.14 = (f32[18,90,1]{1,2,0:T(1,128)S(1)}, f32[18,90,1]{1,2,0:T(1,128)S(1)}, u32[]{:S(2)}, u32[]{:S(2)}) collective-permute-start(f32[18,90,1]{1,2,0:T(1,128)S(1)} %copy.521), channel_id=1, source_target_pairs={{0,1},{1,2},{2,3},{3,0},{4,5},{5,6},{6,7},{7,4},{8,9},{9,10},{10,1... | collective-permute-start | bytes 19448 | tf_op jit(solution)/shard_map/ppermute | solution.py:21
  (107 other events, 183.4 us)
where the time goes:
time: 230 us; the launch traced here: 228 us
  starting transfers between devices  81.2 us (35%)
  local copies, waits for them, and re-layouts  52.9 us (23%)
  other arithmetic  50.4 us (22%)
  waiting for transfers between devices  27.5 us (12%)
  blocking collectives  13.1 us (6%)
  between operations  2.87 us (1%)
    ppermute x8, starting transfers between devices, extended(): after = lax.ppermute(first, axis, down)  41.8 us
    ppermute x8, starting transfers between devices, extended(): before = lax.ppermute(last, axis, up)  17.7 us
    unnamed x1, blocking collectives  13.1 us
    sub x19, other arithmetic, radiate(): 1.0 - albedo_now  12.3 us
    ppermute x8, waiting for transfers between devices, extended(): before = lax.ppermute(last, axis, up)  12 us
    slice x12, local copies, waits for them, and re-layouts, extended(): last = lax.slice_in_dim(x, length - width, length, axis=dim)  11.5 us
    add x4, other arithmetic, per_device(): field_now + mixing_rate * (north_south + east_west - 4.0 * field_now)  9.72 us
    all_to_all x1, waiting for transfers between devices, per_device(): lax.all_to_all(sent_back, 'band', split_axis=0, concat_axis=0, tiled=True)  7.62 us
  transfers between devices with their start and end apart: 20, of which 9 were waited for; matrix products, arithmetic and copies ran while one was open for 17% of the time, Pallas kernels for 0%

commit v1 on v0

v1 whole, which is shorter than its diff:
```python
import jax
import jax.numpy as jnp
from jax import lax
from jax.experimental import pallas as pl
from jax.experimental.pallas import tpu as pltpu
from jax.sharding import PartitionSpec as P

DIFF_STEPS = 4
HALO = 4
EDGE = 16
SUB = 8
F32 = jnp.float32
BF16 = jnp.bfloat16
base_loss = 0.005
step_scale = 0.2**DIFF_STEPS


def vmem():
    return pl.BlockSpec(memory_space=pltpu.VMEM)


def smem():
    return pl.BlockSpec(memory_space=pltpu.SMEM)


def radiate_kernel(
    weight_ref, lit_ref, depth_ref, albedo_ref, sun_ref, anomaly_ref,
    heat_ref, field_ref, top_ref, bottom_ref,
    spread_ref, ratio_ref, swept_ref, extinct_ref,
):
    rows, levels, points, width = depth_ref.shape
    per_level = rows * points
    halves = rows // SUB
    chains = halves * points
    sun = sun_ref[...].astype(F32)
    row_ids = lax.broadcasted_iota(jnp.int32, (rows, width), 0)
    lit = jnp.zeros((rows, width), jnp.int32)
    for row in range(rows):
        lit = jnp.where(row_ids == row, lit_ref[row], lit)
    sun = jnp.where(lit == 1, sun, 0.0)
    suns = [sun[h * SUB:(h + 1) * SUB] for h in range(halves)]

    def spread(level):
        for row in range(rows):
            spread_ref[pl.ds(level * per_level + points * row, points), :] = (
                depth_ref[row, level].astype(F32)
            )

    def depth_of(level, half, point):
        start = level * per_level + half * SUB * points + point
        return spread_ref[pl.ds(start, SUB, stride=points), :]

    def albedo_of(level):
        both = albedo_ref[level].astype(F32)
        return [both[h * SUB:(h + 1) * SUB] for h in range(halves)]

    def place(level, chain):
        return pl.ds(pl.multiple_of(level * per_level + chain * SUB, SUB), SUB)

    zero = jnp.zeros((SUB, width), F32)
    one = jnp.ones((SUB, width), F32)

    def down(level, carry):
        link_prev, albedo_now, depth, light, ratio, swept = carry
        last = level == levels - 1
        following = jnp.where(last, level, level + 1)
        spread(following)
        albedo_next = albedo_of(following)
        out = ([], [], [], [], [])
        for half in range(halves):
            albedo = albedo_now[half]
            before = link_prev[half]
            link = jnp.where(last, 0.0, albedo * albedo_next[half])
            slope = 2.0 * (1.0 - albedo)
            level_part = base_loss + before + link
            for point in range(points):
                chain = half * points + point
                layer = depth_of(level, half, point)
                depth_new = depth[chain] + layer
                light_new = jnp.exp(depth_new * -2.0)
                extinct = suns[half] * (light[chain] - light_new)
                inverse = 1.0 / (level_part + slope * layer - before * ratio[chain])
                ratio_new = link * inverse
                swept_new = (albedo * extinct + before * swept[chain]) * inverse
                where = place(level, chain)
                ratio_ref[where, :] = ratio_new
                swept_ref[where, :] = swept_new
                extinct_ref[where, :] = extinct
                for item, value in zip(out, (depth_new, light_new, ratio_new, swept_new)):
                    item.append(value)
            out[4].append(link)
        return (
            tuple(out[4]), tuple(albedo_next), tuple(out[0]), tuple(out[1]), tuple(out[2]),
            tuple(out[3]),
        )

    spread(0)
    lax.fori_loop(
        0, levels, down,
        ((zero,) * halves, tuple(albedo_of(0)), (zero,) * chains, (one,) * chains,
         (zero,) * chains, (zero,) * chains),
    )
    weights = [weight_ref[point] for point in range(points)]

    def up(i, flux):
        level = levels - 1 - i
        albedos = albedo_of(level)
        flux_new = []
        fields = []
        for half in range(halves):
            total = None
            for point in range(points):
                chain = half * points + point
                where = place(level, chain)
                diffuse = swept_ref[where, :] + ratio_ref[where, :] * flux[chain]
                flux_new.append(diffuse)
                layer = depth_of(level, half, point)
                term = weights[point] * (extinct_ref[where, :] + (2.0 * layer) * diffuse)
                total = term if total is None else total + term
            heat = (1.0 - albedos[half]) * total
            part = pl.ds(half * SUB, SUB)
            heat_ref[level, part, :] = heat
            field = anomaly_ref[level, part, :] + heat
            field_ref[level, part, :] = field
            fields.append(field)
        top_ref[level] = fields[0][:HALO].astype(BF16)
        bottom_ref[level] = fields[-1][SUB - HALO:].astype(BF16)
        return tuple(flux_new)

    lax.fori_loop(0, levels, up, (zero,) * chains)


def rows_of(field_ref, above_ref, below_ref, level):
    halves = field_ref.shape[1] // SUB
    own = [field_ref[level, pl.ds(h * SUB, SUB), :] for h in range(halves)]
    outer = jnp.concatenate(
        [below_ref[level].astype(F32), above_ref[level].astype(F32)], axis=0
    )
    return own + [outer]


def pack_kernel(field_ref, above_ref, below_ref, packed_ref, sent_ref):
    levels, _, width = field_ref.shape
    per_group = width // EDGE
    lanes = lax.broadcasted_iota(jnp.int32, (SUB, width), 1)

    def group_of(group, count):
        packed = None
        for slot in range(count):
            parts = rows_of(field_ref, above_ref, below_ref, group * per_group + slot)
            moved = [pltpu.roll(x, (EDGE * slot + EDGE // 2) % width, 1) for x in parts]
            if packed is None:
                packed = moved
            else:
                packed = [jnp.where(lanes >= EDGE * slot, m, p) for m, p in zip(moved, packed)]
        for part, value in enumerate(packed):
            packed_ref[group, pl.ds(part * SUB, SUB), :] = value
            sent_ref[group, pl.ds(part * SUB, SUB), :] = value.astype(BF16)

    full = levels // per_group
    lax.fori_loop(0, full, lambda g, c: (group_of(g, per_group), c)[1], 0)
    if levels % per_group:
        group_of(full, levels % per_group)


def around(parts, first, final):
    down = [pltpu.roll(x, 1, 0) for x in parts]
    up = [pltpu.roll(x, SUB - 1, 0) for x in parts]
    count = len(parts)
    return [
        jnp.where(first, down[i - 1], down[i]) + jnp.where(final, up[(i + 1) % count], up[i])
        for i in range(count)
    ]


def inside(keep_ref, width):
    sub = lax.broadcasted_iota(jnp.int32, (SUB, width), 0)
    keep = jnp.where(sub < HALO, keep_ref[1], keep_ref[0]).astype(F32)
    return sub == 0, sub == SUB - 1, keep


def main_kernel(keep_ref, field_ref, above_ref, below_ref, out_ref):
    levels, _, width = field_ref.shape
    first, final, keep = inside(keep_ref, width)

    def one_level(level, carry):
        parts = rows_of(field_ref, above_ref, below_ref, level)
        for _ in range(DIFF_STEPS):
            vertical = around(parts, first, final)
            parts = [
                x + v + (pltpu.roll(x, 1, 1) + pltpu.roll(x, width - 1, 1))
                for x, v in zip(parts, vertical)
            ]
            parts[-1] = parts[-1] * keep
        for half, value in enumerate(parts[:-1]):
            out_ref[level, pl.ds(half * SUB, SUB), :] = value * step_scale
        return carry

    lax.fori_loop(0, levels, one_level, 0)


def edge_kernel(keep_ref, packed_ref, west_ref, east_ref, main_ref, out_ref):
    levels, rows, width = main_ref.shape
    per_group = width // EDGE
    halves = rows // SUB
    first, final, keep = inside(keep_ref, width)
    lanes = lax.broadcasted_iota(jnp.int32, (SUB, width), 1)
    column = lanes % EDGE
    mid = EDGE // 2
    last_own = column == mid - 1
    first_own = column == mid
    touched = (lanes < HALO) | (lanes >= width - HALO)

    def group_of(group, count):
        own, other = [], []
        for part in range(halves + 1):
            where = pl.ds(part * SUB, SUB)
            own.append(packed_ref[group, where, :])
            other.append(
                jnp.where(
                    column < mid,
                    west_ref[group, where, :].astype(F32),
                    east_ref[group, where, :].astype(F32),
                )
            )
        for _ in range(DIFF_STEPS):
            own_rows = around(own, first, final)
            other_rows = around(other, first, final)
            own_new, other_new = [], []
            for x, y, v, u in zip(own, other, own_rows, other_rows):
                xe, ye = pltpu.roll(x, width - 1, 1), pltpu.roll(y, width - 1, 1)
                xw, yw = pltpu.roll(x, 1, 1), pltpu.roll(y, 1, 1)
                own_new.append(
                    x + v + (jnp.where(first_own, yw, xw) + jnp.where(last_own, ye, xe))
                )
                other_new.append(
                    y + u + (jnp.where(first_own, xw, yw) + jnp.where(last_own, xe, ye))
                )
            own, other = own_new, other_new
            own[-1] = own[-1] * keep
            other[-1] = other[-1] * keep
        for half in range(halves):
            scaled = own[half] * step_scale
            for slot in range(count):
                moved = pltpu.roll(scaled, (width - EDGE * slot - mid) % width, 1)
                level = group * per_group + slot
                where = pl.ds(half * SUB, SUB)
                out_ref[level, where, :] = jnp.where(touched, moved, main_ref[level, where, :])

    full = levels // per_group
    lax.fori_loop(0, full, lambda g, c: (group_of(g, per_group), c)[1], 0)
    if levels % per_group:
        group_of(full, levels % per_group)


def per_device(optical_depth, albedo, insolation, sunlit, point_weight, anomaly):
    rows, levels, points, width = optical_depth.shape
    planes = jax.ShapeDtypeStruct((levels, rows, width), F32)
    edges = jax.ShapeDtypeStruct((levels, HALO, width), BF16)
    sweep = pltpu.VMEM((levels * rows * points, width), F32)
    heat, field, top, bottom = pl.pallas_call(
        radiate_kernel,
        in_specs=[smem(), smem(), vmem(), vmem(), vmem(), vmem()],
        out_specs=[vmem()] * 4,
        out_shape=[planes, planes, edges, edges],
        scratch_shapes=[sweep] * 4,
        name="radiate",
    )(
        point_weight, sunlit.reshape(rows), optical_depth, jnp.swapaxes(albedo, 0, 1), insolation,
        jnp.swapaxes(anomaly, 0, 1),
    )
    tiles = lax.axis_size("tiles")
    here = lax.axis_index("tiles")
    down = [(i, i + 1) for i in range(tiles - 1)]
    above = lax.ppermute(bottom, "tiles", down)
    below = lax.ppermute(top, "tiles", [(j, i) for i, j in down])
    keep = jnp.stack([here > 0, here < tiles - 1]).astype(jnp.int32)
    groups = -(-levels * EDGE // width)
    side = (groups, rows + SUB, width)
    packed, sent = pl.pallas_call(
        pack_kernel,
        in_specs=[vmem()] * 3,
        out_specs=[vmem()] * 2,
        out_shape=[jax.ShapeDtypeStruct(side, F32), jax.ShapeDtypeStruct(side, BF16)],
        name="pack",
    )(field, above, below)
    bands = lax.axis_size("band")
    east = [(i, (i + 1) % bands) for i in range(bands)]
    from_west = lax.ppermute(sent, "band", east)
    from_east = lax.ppermute(sent, "band", [(j, i) for i, j in east])
    inner = pl.pallas_call(
        main_kernel,
        in_specs=[smem()] + [vmem()] * 3,
        out_specs=vmem(),
        out_shape=planes,
        name="inner",
    )(keep, field, above, below)
    smoothed = pl.pallas_call(
        edge_kernel,
        in_specs=[smem()] + [vmem()] * 4,
        out_specs=vmem(),
        out_shape=planes,
        input_output_aliases={4: 0},
        name="edge",
    )(keep, packed, from_west, from_east, inner)
    return jnp.swapaxes(heat, 0, 1), jnp.swapaxes(smoothed, 0, 1)


def solution(mesh):
    placed = (
        P("tiles", None, None, "band"),
        P("tiles", None, "band"),
        P("tiles", "band"),
        P("tiles", "band"),
        P(),
        P("tiles", None, "band"),
    )
    return jax.shard_map(
        per_device,
        mesh=mesh,
        in_specs=placed,
        out_specs=(P("tiles", None, "band"), P("tiles", None, "band")),
        check_vma=False,
    )
```

time: 230 us -> 73.9 us (0.32)
  the two profiles are of different devices: /device:TPU:2 before, /device:TPU:54 now
where the time goes in v1:
time: 73.9 us; the launch traced here: 73.6 us
  Pallas kernels  44.8 us (61%)
  starting transfers between devices  23.8 us (32%)
  waiting for transfers between devices  2.44 us (3%)
  local copies, waits for them, and re-layouts  1.28 us (2%)
    pallas_call x1, Pallas kernels, per_device(): pl.pallas_call(main_kernel, in_specs=[smem()] + [vmem()] * 3, out_specs=v...  27.7 us
    ppermute x1, starting transfers between devices, per_device(): below = lax.ppermute(top, 'tiles', [(j, i) for i, j in down])  14.8 us
    pallas_call x1, Pallas kernels, per_device(): pl.pallas_call(radiate_kernel, in_specs=[smem(), smem(), vmem(), vmem(),...  7.56 us
    pallas_call x1, Pallas kernels, per_device(): pl.pallas_call(edge_kernel, in_specs=[smem()] + [vmem()] * 4, out_specs=v...  6.64 us
    ppermute x1, starting transfers between devices, per_device(): from_west = lax.ppermute(sent, 'band', east)  4.32 us
    pallas_call x1, Pallas kernels, per_device(): pl.pallas_call(pack_kernel, in_specs=[vmem()] * 3, out_specs=[vmem()] * 2...  2.94 us
    ppermute x1, starting transfers between devices, per_device(): from_east = lax.ppermute(sent, 'band', [(j, i) for i, j in east])  2.72 us
    ppermute x1, waiting for transfers between devices, per_device(): below = lax.ppermute(top, 'tiles', [(j, i) for i, j in down])  1.94 us
  transfers between devices with their start and end apart: 4, of which 2 were waited for; matrix products, arithmetic and copies ran while one was open for 1% of the time, Pallas kernels for 38%

profile of v1, /device:TPU:54, one launch (start us, length us, event | category | flops | bytes accessed | tf_op | source)
XLA Modules:
  0.0 73.6 jit_solution(13864245919622661218)
XLA Ops:
  0.6 7.6 %radiate.1 = (f32[90,16,128]{2,1,0:T(8,128)}, f32[90,16,128]{2,1,0:T(8,128)}, bf16[90,4,128]{2,1,0:T(4,128)(2,1)}, bf16[90,4,128]{2,1,0:T(4,128)(2,1)}) custom-call(f32[4]{0:T(128)} %weight_ref.1, s32[16]{0:T(128)} %bitcast.10, bf16[16,90,4,128]{3,2,1,0:T(4,128)(2,1)} %depth_ref.1, bf16[90,16,128]{2,1,0:T(8,128)(2,1)} %bitcast.9, bf16[16,128]{1,0:T(8,128)(2,1)} %sun_ref.1, ...), custom_call_target="tpu_custom_call" | custom-call | tf_op jit(solution)/shard_map/radiate/pallas_call | solution.py:261
  8.2 1.9 %collective-permute-start = (bf16[90,4,128]{2,1,0:T(4,128)(2,1)}, bf16[90,4,128]{2,1,0:T(4,128)(2,1)S(1)}, u32[]{:S(2)}, u32[]{:S(2)}) collective-permute-start(bf16[90,4,128]{2,1,0:T(4,128)(2,1)} %get-tuple-element.10), channel_id=1, source_target_pairs={{0,4},{4,8},{8,12},{12,16},{16,20},{20,24},{24,28},{28,32},{32,36}... | collective-permute-start | bytes 276488 | tf_op jit(solution)/shard_map/ppermute | solution.py:275
  10.1 14.8 %collective-permute-start.1 = (bf16[90,4,128]{2,1,0:T(4,128)(2,1)}, bf16[90,4,128]{2,1,0:T(4,128)(2,1)S(1)}, u32[]{:S(2)}, u32[]{:S(2)}) collective-permute-start(bf16[90,4,128]{2,1,0:T(4,128)(2,1)} %get-tuple-element.11), channel_id=1, source_target_pairs={{4,0},{8,4},{12,8},{16,12},{20,16},{24,20},{28,24},{32,28},{36,32}... | collective-permute-start | bytes 276488 | tf_op jit(solution)/shard_map/ppermute | solution.py:276
  24.9 0.5 collective-permute-done.above_ref
  25.4 0.0 copy-start
  25.4 1.9 %collective-permute-done.1.below_ref = bf16[90,4,128]{2,1,0:T(4,128)(2,1)S(1)} collective-permute-done((bf16[90,4,128]{2,1,0:T(4,128)(2,1)}, bf16[90,4,128]{2,1,0:T(4,128)(2,1)S(1)}, u32[]{:S(2)}, u32[]{:S(2)}) %collective-permute-start.1) | collective-permute-done | bytes 92192 | tf_op jit(solution)/shard_map/ppermute | solution.py:276
  27.4 0.0 copy-start.1
  27.4 0.0 copy-done
  27.4 0.6 copy-done.1
  28.0 2.9 %pack.1 = (f32[12,24,128]{2,1,0:T(8,128)}, bf16[12,24,128]{2,1,0:T(8,128)(2,1)}) custom-call(f32[90,16,128]{2,1,0:T(8,128)} %get-tuple-element.9.field_ref, bf16[90,4,128]{2,1,0:T(4,128)(2,1)} %copy-done, bf16[90,4,128]{2,1,0:T(4,128)(2,1)} %copy-done.1), custom_call_target="tpu_custom_call" | custom-call | tf_op jit(solution)/shard_map/pack/pallas_call | solution.py:280
  31.0 2.7 %collective-permute-start.3 = (bf16[12,24,128]{2,1,0:T(8,128)(2,1)}, bf16[12,24,128]{2,1,0:T(8,128)(2,1)S(1)}, u32[]{:S(2)}, u32[]{:S(2)}) collective-permute-start(bf16[12,24,128]{2,1,0:T(8,128)(2,1)} %get-tuple-element.13), channel_id=1, source_target_pairs={{1,0},{2,1},{3,2},{0,3},{5,4},{6,5},{7,6},{4,7},{9,8},{10,9},{11,1... | collective-permute-start | bytes 221192 | tf_op jit(solution)/shard_map/ppermute | solution.py:290
  33.7 4.3 %collective-permute-start.2 = (bf16[12,24,128]{2,1,0:T(8,128)(2,1)}, bf16[12,24,128]{2,1,0:T(8,128)(2,1)S(1)}, u32[]{:S(2)}, u32[]{:S(2)}) collective-permute-start(bf16[12,24,128]{2,1,0:T(8,128)(2,1)} %get-tuple-element.13), channel_id=1, source_target_pairs={{0,1},{1,2},{2,3},{3,0},{4,5},{5,6},{6,7},{7,4},{8,9},{9,10},{10,1... | collective-permute-start | bytes 221192 | tf_op jit(solution)/shard_map/ppermute | solution.py:289
  38.0 0.6 add_convert_fusion.keep_ref
  38.6 27.7 %inner.1.main_ref = f32[90,16,128]{2,1,0:T(8,128)} custom-call(s32[2]{0:T(128)} %add_convert_fusion.keep_ref, f32[90,16,128]{2,1,0:T(8,128)} %get-tuple-element.9.field_ref, bf16[90,4,128]{2,1,0:T(4,128)(2,1)} %copy-done, bf16[90,4,128]{2,1,0:T(4,128)(2,1)} %copy-done.1), custom_call_target="tpu_custom_call" | custom-call | tf_op jit(solution)/shard_map/inner/pallas_call | solution.py:291
  66.3 0.0 collective-permute-done.3.east_ref
  66.3 0.0 copy-start.2
  66.3 0.0 collective-permute-done.2.west_ref
  66.3 0.0 copy-start.3
  66.3 0.6 copy-done.2
  66.9 0.0 copy-done.3
  67.0 6.6 %edge.1 = f32[90,16,128]{2,1,0:T(8,128)} custom-call(s32[2]{0:T(128)} %add_convert_fusion.keep_ref, f32[12,24,128]{2,1,0:T(8,128)} %get-tuple-element.12.packed_ref, bf16[12,24,128]{2,1,0:T(8,128)(2,1)} %copy-done.3, bf16[12,24,128]{2,1,0:T(8,128)(2,1)} %copy-done.2, f32[90,16,128]{2,1,0:T(8,128)} %inner.1.main_ref), custom_call_target="tpu_custom_call", output_to_operand_aliasing={{}: (4, {})} | custom-call | tf_op jit(solution)/shard_map/edge/pallas_call | solution.py:298
Async XLA Ops:
  8.2 17.2 %collective-permute-start = (bf16[90,4,128]{2,1,0:T(4,128)(2,1)}, bf16[90,4,128]{2,1,0:T(4,128)(2,1)S(1)}, u32[]{:S(2)}, u32[]{:S(2)}) collective-permute-start(bf16[90,4,128]{2,1,0:T(4,128)(2,1)} %get-tuple-element.10), channel_id=1, source_target_pairs={{0,4},{4,8},{8,12},{12,16},{16,20},{20,24},{24,28},{28,32},{32,36}... | collective-permute-start | bytes 276488 | tf_op jit(solution)/shard_map/ppermute | solution.py:275
  10.1 17.3 %collective-permute-start.1 = (bf16[90,4,128]{2,1,0:T(4,128)(2,1)}, bf16[90,4,128]{2,1,0:T(4,128)(2,1)S(1)}, u32[]{:S(2)}, u32[]{:S(2)}) collective-permute-start(bf16[90,4,128]{2,1,0:T(4,128)(2,1)} %get-tuple-element.11), channel_id=1, source_target_pairs={{4,0},{8,4},{12,8},{16,12},{20,16},{24,20},{28,24},{32,28},{36,32}... | collective-permute-start | bytes 276488 | tf_op jit(solution)/shard_map/ppermute | solution.py:276
  25.4 2.0 %copy-start = (bf16[90,4,128]{2,1,0:T(4,128)(2,1)}, bf16[90,4,128]{2,1,0:T(4,128)(2,1)S(1)}, u32[]{:S(2)}) copy-start(bf16[90,4,128]{2,1,0:T(4,128)(2,1)S(1)} %collective-permute-done.above_ref) | copy-start | bytes 276484
  27.4 0.6 copy-start.1
  31.0 35.3 %collective-permute-start.3 = (bf16[12,24,128]{2,1,0:T(8,128)(2,1)}, bf16[12,24,128]{2,1,0:T(8,128)(2,1)S(1)}, u32[]{:S(2)}, u32[]{:S(2)}) collective-permute-start(bf16[12,24,128]{2,1,0:T(8,128)(2,1)} %get-tuple-element.13), channel_id=1, source_target_pairs={{1,0},{2,1},{3,2},{0,3},{5,4},{6,5},{7,6},{4,7},{9,8},{10,9},{11,1... | collective-permute-start | bytes 221192 | tf_op jit(solution)/shard_map/ppermute | solution.py:290
  33.7 32.6 %collective-permute-start.2 = (bf16[12,24,128]{2,1,0:T(8,128)(2,1)}, bf16[12,24,128]{2,1,0:T(8,128)(2,1)S(1)}, u32[]{:S(2)}, u32[]{:S(2)}) collective-permute-start(bf16[12,24,128]{2,1,0:T(8,128)(2,1)} %get-tuple-element.13), channel_id=1, source_target_pairs={{0,1},{1,2},{2,3},{3,0},{4,5},{5,6},{6,7},{7,4},{8,9},{9,10},{10,1... | collective-permute-start | bytes 221192 | tf_op jit(solution)/shard_map/ppermute | solution.py:289
  66.3 0.6 copy-start.2
  66.3 0.7 copy-start.3

commit v2 on v1

--- a/solution.py
+++ b/solution.py
@@ -6,6 +6,8 @@
 from jax.sharding import PartitionSpec as P
 
 DIFF_STEPS = 4
+BATCH = 10
+GROUPS = 4
 HALO = 4
 EDGE = 16
 SUB = 8
@@ -183,20 +185,26 @@
     levels, _, width = field_ref.shape
     first, final, keep = inside(keep_ref, width)
 
-    def one_level(level, carry):
-        parts = rows_of(field_ref, above_ref, below_ref, level)
+    def some_levels(block, carry):
+        found = [block * BATCH + i for i in range(BATCH)]
+        sets = [rows_of(field_ref, above_ref, below_ref, level) for level in found]
         for _ in range(DIFF_STEPS):
-            vertical = around(parts, first, final)
-            parts = [
-                x + v + (pltpu.roll(x, 1, 1) + pltpu.roll(x, width - 1, 1))
-                for x, v in zip(parts, vertical)
-            ]
-            parts[-1] = parts[-1] * keep
-        for half, value in enumerate(parts[:-1]):
-            out_ref[level, pl.ds(half * SUB, SUB), :] = value * step_scale
+            new = []
+            for parts in sets:
+                vertical = around(parts, first, final)
+                parts = [
+                    x + v + (pltpu.roll(x, 1, 1) + pltpu.roll(x, width - 1, 1))
+                    for x, v in zip(parts, vertical)
+                ]
+                parts[-1] = parts[-1] * keep
+                new.append(parts)
+            sets = new
+        for level, parts in zip(found, sets):
+            for half, value in enumerate(parts[:-1]):
+                out_ref[level, pl.ds(half * SUB, SUB), :] = value * step_scale
         return carry
 
-    lax.fori_loop(0, levels, one_level, 0)
+    lax.fori_loop(0, levels // BATCH, some_levels, 0)
 
 
 def edge_kernel(keep_ref, packed_ref, west_ref, east_ref, main_ref, out_ref):
@@ -211,46 +219,58 @@
     first_own = column == mid
     touched = (lanes < HALO) | (lanes >= width - HALO)
 
-    def group_of(group, count):
-        own, other = [], []
-        for part in range(halves + 1):
-            where = pl.ds(part * SUB, SUB)
-            own.append(packed_ref[group, where, :])
-            other.append(
-                jnp.where(
-                    column < mid,
-                    west_ref[group, where, :].astype(F32),
-                    east_ref[group, where, :].astype(F32),
+    def block_of(block, counts):
+        groups = [block * GROUPS + i for i in range(len(counts))]
+        sets = []
+        for group in groups:
+            own, other = [], []
+            for part in range(halves + 1):
+                where = pl.ds(part * SUB, SUB)
+                own.append(packed_ref[group, where, :])
+                other.append(
+                    jnp.where(
+                        column < mid,
+                        west_ref[group, where, :].astype(F32),
+                        east_ref[group, where, :].astype(F32),
+                    )
                 )
-            )
+            sets.append((own, other))
         for _ in range(DIFF_STEPS):
-            own_rows = around(own, first, final)
-            other_rows = around(other, first, final)
-            own_new, other_new = [], []
-            for x, y, v, u in zip(own, other, own_rows, other_rows):
-                xe, ye = pltpu.roll(x, width - 1, 1), pltpu.roll(y, width - 1, 1)
-                xw, yw = pltpu.roll(x, 1, 1), pltpu.roll(y, 1, 1)
-                own_new.append(
-                    x + v + (jnp.where(first_own, yw, xw) + jnp.where(last_own, ye, xe))
-                )
-                other_new.append(
-                    y + u + (jnp.where(first_own, xw, yw) + jnp.where(last_own, xe, ye))
-                )
-            own, other = own_new, other_new
-            own[-1] = own[-1] * keep
-            other[-1] = other[-1] * keep
-        for half in range(halves):
-            scaled = own[half] * step_scale
-            for slot in range(count):
-                moved = pltpu.roll(scaled, (width - EDGE * slot - mid) % width, 1)
-                level = group * per_group + slot
+            new = []
+            for own, other in sets:
+                own_rows = around(own, first, final)
+                other_rows = around(other, first, final)
+                own_new, other_new = [], []
+                for x, y, v, u in zip(own, other, own_rows, other_rows):
+                    xe, ye = pltpu.roll(x, width - 1, 1), pltpu.roll(y, width - 1, 1)
+                    xw, yw = pltpu.roll(x, 1, 1), pltpu.roll(y, 1, 1)
+                    own_new.append(
+                        x + v + (jnp.where(first_own, yw, xw) + jnp.where(last_own, ye, xe))
+                    )
+                    other_new.append(
+                        y + u + (jnp.where(first_own, xw, yw) + jnp.where(last_own, xe, ye))
+                    )
+                own_new[-1] = own_new[-1] * keep
+                other_new[-1] = other_new[-1] * keep
+                new.append((own_new, other_new))
+            sets = new
+        for group, count, (own, _) in zip(groups, counts, sets):
+            for half in range(halves):
+                scaled = own[half] * step_scale
                 where = pl.ds(half * SUB, SUB)
-                out_ref[level, where, :] = jnp.where(touched, moved, main_ref[level, where, :])
+                for slot in range(count):
+                    moved = pltpu.roll(scaled, (width - EDGE * slot - mid) % width, 1)
+                    level = group * per_group + slot
+                    out_ref[level, where, :] = jnp.where(
+                        touched, moved, main_ref[level, where, :]
+                    )
 
     full = levels // per_group
-    lax.fori_loop(0, full, lambda g, c: (group_of(g, per_group), c)[1], 0)
-    if levels % per_group:
-        group_of(full, levels % per_group)
+    counts = [per_group] * full + ([levels % per_group] if levels % per_group else [])
+    blocks = full // GROUPS
+    lax.fori_loop(0, blocks, lambda b, c: (block_of(b, counts[:GROUPS]), c)[1], 0)
+    if counts[blocks * GROUPS:]:
+        block_of(blocks, counts[blocks * GROUPS:])
 
 
 def per_device(optical_depth, albedo, insolation, sunlit, point_weight, anomaly):

time: 73.9 us -> 48.1 us (0.65)
  the two profiles are of different devices: /device:TPU:54 before, /device:TPU:46 now
where the time goes in v2:
time: 48.1 us; the launch traced here: 47.8 us
  starting transfers between devices  23.8 us (49%)
  Pallas kernels  19.1 us (40%)
  waiting for transfers between devices  2.44 us (5%)
  local copies, waits for them, and re-layouts  1.28 us (3%)
  between operations  0.69 us (1%)
  other arithmetic  0.6 us (1%)
    ppermute x1, starting transfers between devices, per_device(): below = lax.ppermute(top, 'tiles', [(j, i) for i, j in down])  14.8 us
    pallas_call x1, Pallas kernels, per_device(): pl.pallas_call(radiate_kernel, in_specs=[smem(), smem(), vmem(), vmem(),...  7.56 us
    pallas_call x1, Pallas kernels, per_device(): pl.pallas_call(main_kernel, in_specs=[smem()] + [vmem()] * 3, out_specs=v...  5.15 us
    ppermute x1, starting transfers between devices, per_device(): from_west = lax.ppermute(sent, 'band', east)  4.32 us
    pallas_call x1, Pallas kernels, per_device(): pl.pallas_call(edge_kernel, in_specs=[smem()] + [vmem()] * 4, out_specs=v...  3.4 us
    pallas_call x1, Pallas kernels, per_device(): pl.pallas_call(pack_kernel, in_specs=[vmem()] * 3, out_specs=[vmem()] * 2...  2.94 us
    ppermute x1, starting transfers between devices, per_device(): from_east = lax.ppermute(sent, 'band', [(j, i) for i, j in east])  2.72 us
    ppermute x1, waiting for transfers between devices, per_device(): below = lax.ppermute(top, 'tiles', [(j, i) for i, j in down])  1.94 us
  transfers between devices with their start and end apart: 4, of which 2 were waited for; matrix products, arithmetic and copies ran while one was open for 1% of the time, Pallas kernels for 11%

profile of v2, /device:TPU:46, one launch (start us, length us, event | category | flops | bytes accessed | tf_op | source)
XLA Modules:
  0.0 47.8 jit_solution(11069212901881756289)
XLA Ops:
  0.6 7.6 %radiate.1 = (f32[90,16,128]{2,1,0:T(8,128)}, f32[90,16,128]{2,1,0:T(8,128)}, bf16[90,4,128]{2,1,0:T(4,128)(2,1)}, bf16[90,4,128]{2,1,0:T(4,128)(2,1)}) custom-call(f32[4]{0:T(128)} %weight_ref.1, s32[16]{0:T(128)} %bitcast.10, bf16[16,90,4,128]{3,2,1,0:T(4,128)(2,1)} %depth_ref.1, bf16[90,16,128]{2,1,0:T(8,128)(2,1)} %bitcast.9, bf16[16,128]{1,0:T(8,128)(2,1)} %sun_ref.1, ...), custom_call_target="tpu_custom_call" | custom-call | tf_op jit(solution)/shard_map/radiate/pallas_call | solution.py:281
  8.2 1.9 %collective-permute-start = (bf16[90,4,128]{2,1,0:T(4,128)(2,1)}, bf16[90,4,128]{2,1,0:T(4,128)(2,1)S(1)}, u32[]{:S(2)}, u32[]{:S(2)}) collective-permute-start(bf16[90,4,128]{2,1,0:T(4,128)(2,1)} %get-tuple-element.10), channel_id=1, source_target_pairs={{0,4},{4,8},{8,12},{12,16},{16,20},{20,24},{24,28},{28,32},{32,36}... | collective-permute-start | bytes 276488 | tf_op jit(solution)/shard_map/ppermute | solution.py:295
  10.1 14.8 %collective-permute-start.1 = (bf16[90,4,128]{2,1,0:T(4,128)(2,1)}, bf16[90,4,128]{2,1,0:T(4,128)(2,1)S(1)}, u32[]{:S(2)}, u32[]{:S(2)}) collective-permute-start(bf16[90,4,128]{2,1,0:T(4,128)(2,1)} %get-tuple-element.11), channel_id=1, source_target_pairs={{4,0},{8,4},{12,8},{16,12},{20,16},{24,20},{28,24},{32,28},{36,32}... | collective-permute-start | bytes 276488 | tf_op jit(solution)/shard_map/ppermute | solution.py:296
  24.9 0.5 %collective-permute-done.above_ref = bf16[90,4,128]{2,1,0:T(4,128)(2,1)S(1)} collective-permute-done((bf16[90,4,128]{2,1,0:T(4,128)(2,1)}, bf16[90,4,128]{2,1,0:T(4,128)(2,1)S(1)}, u32[]{:S(2)}, u32[]{:S(2)}) %collective-permute-start) | collective-permute-done | bytes 92192 | tf_op jit(solution)/shard_map/ppermute | solution.py:295
  25.4 0.0 copy-start
  25.4 1.9 %collective-permute-done.1.below_ref = bf16[90,4,128]{2,1,0:T(4,128)(2,1)S(1)} collective-permute-done((bf16[90,4,128]{2,1,0:T(4,128)(2,1)}, bf16[90,4,128]{2,1,0:T(4,128)(2,1)S(1)}, u32[]{:S(2)}, u32[]{:S(2)}) %collective-permute-start.1) | collective-permute-done | bytes 92192 | tf_op jit(solution)/shard_map/ppermute | solution.py:296
  27.4 0.0 copy-start.1
  27.4 0.0 copy-done
  27.4 0.6 %copy-done.1 = bf16[90,4,128]{2,1,0:T(4,128)(2,1)} copy-done((bf16[90,4,128]{2,1,0:T(4,128)(2,1)}, bf16[90,4,128]{2,1,0:T(4,128)(2,1)S(1)}, u32[]{:S(2)}) %copy-start.1) | copy-done | bytes 92184
  28.0 2.9 %pack.1 = (f32[12,24,128]{2,1,0:T(8,128)}, bf16[12,24,128]{2,1,0:T(8,128)(2,1)}) custom-call(f32[90,16,128]{2,1,0:T(8,128)} %get-tuple-element.9.field_ref, bf16[90,4,128]{2,1,0:T(4,128)(2,1)} %copy-done, bf16[90,4,128]{2,1,0:T(4,128)(2,1)} %copy-done.1), custom_call_target="tpu_custom_call" | custom-call | tf_op jit(solution)/shard_map/pack/pallas_call | solution.py:300
  31.0 2.7 %collective-permute-start.3 = (bf16[12,24,128]{2,1,0:T(8,128)(2,1)}, bf16[12,24,128]{2,1,0:T(8,128)(2,1)S(1)}, u32[]{:S(2)}, u32[]{:S(2)}) collective-permute-start(bf16[12,24,128]{2,1,0:T(8,128)(2,1)} %get-tuple-element.13), channel_id=1, source_target_pairs={{1,0},{2,1},{3,2},{0,3},{5,4},{6,5},{7,6},{4,7},{9,8},{10,9},{11,1... | collective-permute-start | bytes 221192 | tf_op jit(solution)/shard_map/ppermute | solution.py:310
  33.7 4.3 %collective-permute-start.2 = (bf16[12,24,128]{2,1,0:T(8,128)(2,1)}, bf16[12,24,128]{2,1,0:T(8,128)(2,1)S(1)}, u32[]{:S(2)}, u32[]{:S(2)}) collective-permute-start(bf16[12,24,128]{2,1,0:T(8,128)(2,1)} %get-tuple-element.13), channel_id=1, source_target_pairs={{0,1},{1,2},{2,3},{3,0},{4,5},{5,6},{6,7},{7,4},{8,9},{9,10},{10,1... | collective-permute-start | bytes 221192 | tf_op jit(solution)/shard_map/ppermute | solution.py:309
  38.0 0.6 %add_convert_fusion.keep_ref = s32[2]{0:T(128)} fusion(pred[1]{0:T(512)(128)(4,1)} %bitcast.5, pred[1]{0:T(512)(128)(4,1)} %bitcast.4), kind=kLoop, calls=%fused_computation | loop fusion | flops 4 | bytes 10 | tf_op jit(solution)/shard_map/convert_element_type | solution.py:297
  38.6 5.1 %inner.1.main_ref = f32[90,16,128]{2,1,0:T(8,128)} custom-call(s32[2]{0:T(128)} %add_convert_fusion.keep_ref, f32[90,16,128]{2,1,0:T(8,128)} %get-tuple-element.9.field_ref, bf16[90,4,128]{2,1,0:T(4,128)(2,1)} %copy-done, bf16[90,4,128]{2,1,0:T(4,128)(2,1)} %copy-done.1), custom_call_target="tpu_custom_call" | custom-call | tf_op jit(solution)/shard_map/inner/pallas_call | solution.py:311
  43.8 0.0 collective-permute-done.3.east_ref
  43.8 0.0 copy-start.2
  43.8 0.0 collective-permute-done.2.west_ref
  43.8 0.0 copy-start.3
  43.8 0.6 %copy-done.2 = bf16[12,24,128]{2,1,0:T(8,128)(2,1)} copy-done((bf16[12,24,128]{2,1,0:T(8,128)(2,1)}, bf16[12,24,128]{2,1,0:T(8,128)(2,1)S(1)}, u32[]{:S(2)}) %copy-start.2) | copy-done | bytes 73752
  44.4 0.0 copy-done.3
  44.4 3.4 %edge.1 = f32[90,16,128]{2,1,0:T(8,128)} custom-call(s32[2]{0:T(128)} %add_convert_fusion.keep_ref, f32[12,24,128]{2,1,0:T(8,128)} %get-tuple-element.12.packed_ref, bf16[12,24,128]{2,1,0:T(8,128)(2,1)} %copy-done.3, bf16[12,24,128]{2,1,0:T(8,128)(2,1)} %copy-done.2, f32[90,16,128]{2,1,0:T(8,128)} %inner.1.main_ref), custom_call_target="tpu_custom_call", output_to_operand_aliasing={{}: (4, {})} | custom-call | tf_op jit(solution)/shard_map/edge/pallas_call | solution.py:318
Async XLA Ops:
  8.2 17.2 %collective-permute-start = (bf16[90,4,128]{2,1,0:T(4,128)(2,1)}, bf16[90,4,128]{2,1,0:T(4,128)(2,1)S(1)}, u32[]{:S(2)}, u32[]{:S(2)}) collective-permute-start(bf16[90,4,128]{2,1,0:T(4,128)(2,1)} %get-tuple-element.10), channel_id=1, source_target_pairs={{0,4},{4,8},{8,12},{12,16},{16,20},{20,24},{24,28},{28,32},{32,36}... | collective-permute-start | bytes 276488 | tf_op jit(solution)/shard_map/ppermute | solution.py:295
  10.1 17.3 %collective-permute-start.1 = (bf16[90,4,128]{2,1,0:T(4,128)(2,1)}, bf16[90,4,128]{2,1,0:T(4,128)(2,1)S(1)}, u32[]{:S(2)}, u32[]{:S(2)}) collective-permute-start(bf16[90,4,128]{2,1,0:T(4,128)(2,1)} %get-tuple-element.11), channel_id=1, source_target_pairs={{4,0},{8,4},{12,8},{16,12},{20,16},{24,20},{28,24},{32,28},{36,32}... | collective-permute-start | bytes 276488 | tf_op jit(solution)/shard_map/ppermute | solution.py:296
  25.4 2.0 %copy-start = (bf16[90,4,128]{2,1,0:T(4,128)(2,1)}, bf16[90,4,128]{2,1,0:T(4,128)(2,1)S(1)}, u32[]{:S(2)}) copy-start(bf16[90,4,128]{2,1,0:T(4,128)(2,1)S(1)} %collective-permute-done.above_ref) | copy-start | bytes 276484
  27.4 0.6 %copy-start.1 = (bf16[90,4,128]{2,1,0:T(4,128)(2,1)}, bf16[90,4,128]{2,1,0:T(4,128)(2,1)S(1)}, u32[]{:S(2)}) copy-start(bf16[90,4,128]{2,1,0:T(4,128)(2,1)S(1)} %collective-permute-done.1.below_ref) | copy-start | bytes 276484
  31.0 12.8 %collective-permute-start.3 = (bf16[12,24,128]{2,1,0:T(8,128)(2,1)}, bf16[12,24,128]{2,1,0:T(8,128)(2,1)S(1)}, u32[]{:S(2)}, u32[]{:S(2)}) collective-permute-start(bf16[12,24,128]{2,1,0:T(8,128)(2,1)} %get-tuple-element.13), channel_id=1, source_target_pairs={{1,0},{2,1},{3,2},{0,3},{5,4},{6,5},{7,6},{4,7},{9,8},{10,9},{11,1... | collective-permute-start | bytes 221192 | tf_op jit(solution)/shard_map/ppermute | solution.py:310
  33.7 10.1 %collective-permute-start.2 = (bf16[12,24,128]{2,1,0:T(8,128)(2,1)}, bf16[12,24,128]{2,1,0:T(8,128)(2,1)S(1)}, u32[]{:S(2)}, u32[]{:S(2)}) collective-permute-start(bf16[12,24,128]{2,1,0:T(8,128)(2,1)} %get-tuple-element.13), channel_id=1, source_target_pairs={{0,1},{1,2},{2,3},{3,0},{4,5},{5,6},{6,7},{7,4},{8,9},{9,10},{10,1... | collective-permute-start | bytes 221192 | tf_op jit(solution)/shard_map/ppermute | solution.py:309
  43.8 0.6 %copy-start.2 = (bf16[12,24,128]{2,1,0:T(8,128)(2,1)}, bf16[12,24,128]{2,1,0:T(8,128)(2,1)S(1)}, u32[]{:S(2)}) copy-start(bf16[12,24,128]{2,1,0:T(8,128)(2,1)S(1)} %collective-permute-done.3.east_ref) | copy-start | bytes 221188
  43.8 0.7 %copy-start.3 = (bf16[12,24,128]{2,1,0:T(8,128)(2,1)}, bf16[12,24,128]{2,1,0:T(8,128)(2,1)S(1)}, u32[]{:S(2)}) copy-start(bf16[12,24,128]{2,1,0:T(8,128)(2,1)S(1)} %collective-permute-done.2.west_ref) | copy-start | bytes 221188

commit v3 on v2

--- a/solution.py
+++ b/solution.py
@@ -1,3 +1,6 @@
+import functools
+import math
+
 import jax
 import jax.numpy as jnp
 from jax import lax
@@ -8,6 +11,9 @@
 DIFF_STEPS = 4
 BATCH = 10
 GROUPS = 4
+UNROLL_DOWN = 3
+UNROLL_UP = 6
+LIGHT_RATE = -2.0 * math.log2(math.e)
 HALO = 4
 EDGE = 16
 SUB = 8
@@ -26,8 +32,8 @@
 
 
 def radiate_kernel(
-    weight_ref, lit_ref, depth_ref, albedo_ref, sun_ref, anomaly_ref,
-    heat_ref, field_ref, top_ref, bottom_ref,
+    here_ref, weight_ref, lit_ref, depth_ref, albedo_ref, sun_ref, anomaly_ref,
+    heat_ref, field_ref, pair_ref, step_ref,
     spread_ref, ratio_ref, swept_ref, extinct_ref,
 ):
     rows, levels, points, width = depth_ref.shape
@@ -79,7 +85,7 @@
                 chain = half * points + point
                 layer = depth_of(level, half, point)
                 depth_new = depth[chain] + layer
-                light_new = jnp.exp(depth_new * -2.0)
+                light_new = jnp.exp2(depth_new * LIGHT_RATE)
                 extinct = suns[half] * (light[chain] - light_new)
                 inverse = 1.0 / (level_part + slope * layer - before * ratio[chain])
                 ratio_new = link * inverse
@@ -101,7 +107,9 @@
         0, levels, down,
         ((zero,) * halves, tuple(albedo_of(0)), (zero,) * chains, (one,) * chains,
          (zero,) * chains, (zero,) * chains),
+        unroll=UNROLL_DOWN,
     )
+    even = here_ref[0] % 2 == 0
     weights = [weight_ref[point] for point in range(points)]
 
     def up(i, flux):
@@ -125,44 +133,76 @@
             field = anomaly_ref[level, part, :] + heat
             field_ref[level, part, :] = field
             fields.append(field)
-        top_ref[level] = fields[0][:HALO].astype(BF16)
-        bottom_ref[level] = fields[-1][SUB - HALO:].astype(BF16)
+        top, bottom = fields[0][:HALO], fields[-1][SUB - HALO:]
+        pair_ref[level] = jnp.where(even, bottom, top).astype(BF16)
+        step_ref[level] = jnp.where(even, top, bottom).astype(BF16)
         return tuple(flux_new)
 
-    lax.fori_loop(0, levels, up, (zero,) * chains)
-
-
-def rows_of(field_ref, above_ref, below_ref, level):
-    halves = field_ref.shape[1] // SUB
-    own = [field_ref[level, pl.ds(h * SUB, SUB), :] for h in range(halves)]
-    outer = jnp.concatenate(
-        [below_ref[level].astype(F32), above_ref[level].astype(F32)], axis=0
-    )
-    return own + [outer]
-
-
-def pack_kernel(field_ref, above_ref, below_ref, packed_ref, sent_ref):
-    levels, _, width = field_ref.shape
+    lax.fori_loop(0, levels, up, (zero,) * chains, unroll=UNROLL_UP)
+
+
+def outer_rows(here_ref, pair_ref, step_ref, level):
+    pair, step = pair_ref[level].astype(F32), step_ref[level].astype(F32)
+    even = here_ref[0] % 2 == 0
+    below = jnp.where(even, pair, step)
+    above = jnp.where(even, step, pair)
+    return jnp.concatenate([below, above], axis=0)
+
+
+def pack_levels(lanes, parts):
+    width = lanes.shape[1]
+    packed = None
+    for slot, part in enumerate(parts):
+        moved = pltpu.roll(part, (EDGE * slot + EDGE // 2) % width, 1)
+        packed = moved if packed is None else jnp.where(lanes >= EDGE * slot, moved, packed)
+    return packed
+
+
+def each_block(levels, per_group, body):
+    full = levels // per_group
+    counts = [per_group] * full + ([levels % per_group] if levels % per_group else [])
+    blocks = full // GROUPS
+    lax.fori_loop(0, blocks, lambda b, c: (body(b, counts[:GROUPS]), c)[1], 0)
+    if counts[blocks * GROUPS:]:
+        body(blocks, counts[blocks * GROUPS:])
+
+
+def pack_own_kernel(field_ref, packed_ref):
+    levels, rows, width = field_ref.shape
     per_group = width // EDGE
     lanes = lax.broadcasted_iota(jnp.int32, (SUB, width), 1)
 
-    def group_of(group, count):
-        packed = None
-        for slot in range(count):
-            parts = rows_of(field_ref, above_ref, below_ref, group * per_group + slot)
-            moved = [pltpu.roll(x, (EDGE * slot + EDGE // 2) % width, 1) for x in parts]
-            if packed is None:
-                packed = moved
-            else:
-                packed = [jnp.where(lanes >= EDGE * slot, m, p) for m, p in zip(moved, packed)]
-        for part, value in enumerate(packed):
-            packed_ref[group, pl.ds(part * SUB, SUB), :] = value
-            sent_ref[group, pl.ds(part * SUB, SUB), :] = value.astype(BF16)
-
-    full = levels // per_group
-    lax.fori_loop(0, full, lambda g, c: (group_of(g, per_group), c)[1], 0)
-    if levels % per_group:
-        group_of(full, levels % per_group)
+    def block_of(block, counts):
+        for i, count in enumerate(counts):
+            group = block * GROUPS + i
+            for half in range(rows // SUB):
+                where = pl.ds(half * SUB, SUB)
+                packed_ref[group, where, :] = pack_levels(
+                    lanes, [field_ref[group * per_group + k, where, :] for k in range(count)]
+                )
+
+    each_block(levels, per_group, block_of)
+
+
+def pack_outer_kernel(here_ref, pair_ref, step_ref, own_ref, outer_ref, sent_ref):
+    levels, _, width = pair_ref.shape
+    rows = own_ref.shape[1]
+    per_group = width // EDGE
+    lanes = lax.broadcasted_iota(jnp.int32, (SUB, width), 1)
+
+    def block_of(block, counts):
+        for i, count in enumerate(counts):
+            group = block * GROUPS + i
+            packed = pack_levels(
+                lanes,
+                [outer_rows(here_ref, pair_ref, step_ref, group * per_group + k)
+                 for k in range(count)],
+            )
+            outer_ref[group] = packed
+            sent_ref[group, pl.ds(rows, SUB), :] = packed.astype(BF16)
+            sent_ref[group, pl.ds(0, rows), :] = own_ref[group].astype(BF16)
+
+    each_block(levels, per_group, block_of)
 
 
 def around(parts, first, final):
@@ -175,19 +215,26 @@
     ]
 
 
-def inside(keep_ref, width):
+def inside(here_ref, tiles, width):
     sub = lax.broadcasted_iota(jnp.int32, (SUB, width), 0)
-    keep = jnp.where(sub < HALO, keep_ref[1], keep_ref[0]).astype(F32)
-    return sub == 0, sub == SUB - 1, keep
-
-
-def main_kernel(keep_ref, field_ref, above_ref, below_ref, out_ref):
-    levels, _, width = field_ref.shape
-    first, final, keep = inside(keep_ref, width)
+    tile = here_ref[0]
+    keep = jnp.where(
+        sub < HALO, (tile < tiles - 1).astype(jnp.int32), (tile > 0).astype(jnp.int32)
+    )
+    return sub == 0, sub == SUB - 1, keep.astype(F32)
+
+
+def main_kernel(tiles, here_ref, field_ref, pair_ref, step_ref, out_ref):
+    levels, rows, width = field_ref.shape
+    first, final, keep = inside(here_ref, tiles, width)
 
     def some_levels(block, carry):
         found = [block * BATCH + i for i in range(BATCH)]
-        sets = [rows_of(field_ref, above_ref, below_ref, level) for level in found]
+        sets = [
+            [field_ref[level, pl.ds(h * SUB, SUB), :] for h in range(rows // SUB)]
+            + [outer_rows(here_ref, pair_ref, step_ref, level)]
+            for level in found
+        ]
         for _ in range(DIFF_STEPS):
             new = []
             for parts in sets:
@@ -207,16 +254,20 @@
     lax.fori_loop(0, levels // BATCH, some_levels, 0)
 
 
-def edge_kernel(keep_ref, packed_ref, west_ref, east_ref, main_ref, out_ref):
+def edge_kernel(
+    tiles, here_ref, side_ref, own_ref, outer_ref, near_ref, far_ref, main_ref, out_ref
+):
     levels, rows, width = main_ref.shape
     per_group = width // EDGE
     halves = rows // SUB
-    first, final, keep = inside(keep_ref, width)
+    first, final, keep = inside(here_ref, tiles, width)
+    swapped = side_ref[0] % 2 == 1
     lanes = lax.broadcasted_iota(jnp.int32, (SUB, width), 1)
     column = lanes % EDGE
     mid = EDGE // 2
     last_own = column == mid - 1
     first_own = column == mid
+    from_near = (column < mid).astype(jnp.int32) == swapped.astype(jnp.int32)
     touched = (lanes < HALO) | (lanes >= width - HALO)
 
     def block_of(block, counts):
@@ -226,14 +277,10 @@
             own, other = [], []
             for part in range(halves + 1):
                 where = pl.ds(part * SUB, SUB)
-                own.append(packed_ref[group, where, :])
-                other.append(
-                    jnp.where(
-                        column < mid,
-                        west_ref[group, where, :].astype(F32),
-                        east_ref[group, where, :].astype(F32),
-                    )
-                )
+                own.append(own_ref[group, where, :] if part < halves else outer_ref[group])
+                near = near_ref[group, where, :].astype(F32)
+                far = far_ref[group, where, :].astype(F32)
+                other.append(jnp.where(from_near, near, far))
             sets.append((own, other))
         for _ in range(DIFF_STEPS):
             new = []
@@ -265,64 +312,77 @@
                         touched, moved, main_ref[level, where, :]
                     )
 
-    full = levels // per_group
-    counts = [per_group] * full + ([levels % per_group] if levels % per_group else [])
-    blocks = full // GROUPS
-    lax.fori_loop(0, blocks, lambda b, c: (block_of(b, counts[:GROUPS]), c)[1], 0)
-    if counts[blocks * GROUPS:]:
-        block_of(blocks, counts[blocks * GROUPS:])
+    each_block(levels, per_group, block_of)
+
+
+def fast(shape, dtype):
+    return pltpu.VMEM(shape, dtype)
+
+
+def held(x):
+    return pltpu.with_memory_space_constraint(x, pltpu.VMEM)
+
+
+def swaps(size, first, ring):
+    ends = range(first, size if ring else size - 1, 2)
+    return [pair for i in ends for pair in ((i, (i + 1) % size), ((i + 1) % size, i))]
 
 
 def per_device(optical_depth, albedo, insolation, sunlit, point_weight, anomaly):
     rows, levels, points, width = optical_depth.shape
-    planes = jax.ShapeDtypeStruct((levels, rows, width), F32)
-    edges = jax.ShapeDtypeStruct((levels, HALO, width), BF16)
+    tiles, bands = lax.axis_size("tiles"), lax.axis_size("band")
+    here = lax.axis_index("tiles").astype(jnp.int32).reshape(1)
+    side = lax.axis_index("band").astype(jnp.int32).reshape(1)
+    planes = (levels, rows, width)
+    edges = (levels, HALO, width)
+    groups = -(-levels * EDGE // width)
     sweep = pltpu.VMEM((levels * rows * points, width), F32)
-    heat, field, top, bottom = pl.pallas_call(
+    heat, field, pair_edge, step_edge = pl.pallas_call(
         radiate_kernel,
-        in_specs=[smem(), smem(), vmem(), vmem(), vmem(), vmem()],
+        in_specs=[smem(), smem(), smem(), vmem(), vmem(), vmem(), vmem()],
         out_specs=[vmem()] * 4,
-        out_shape=[planes, planes, edges, edges],
+        out_shape=[
+            jax.ShapeDtypeStruct(planes, F32), fast(planes, F32), fast(edges, BF16),
+            fast(edges, BF16),
+        ],
         scratch_shapes=[sweep] * 4,
         name="radiate",
     )(
-        point_weight, sunlit.reshape(rows), optical_depth, jnp.swapaxes(albedo, 0, 1), insolation,
-        jnp.swapaxes(anomaly, 0, 1),
+        here, point_weight, sunlit.reshape(rows), optical_depth, jnp.swapaxes(albedo, 0, 1),
+        insolation, jnp.swapaxes(anomaly, 0, 1),
     )
-    tiles = lax.axis_size("tiles")
-    here = lax.axis_index("tiles")
-    down = [(i, i + 1) for i in range(tiles - 1)]
-    above = lax.ppermute(bottom, "tiles", down)
-    below = lax.ppermute(top, "tiles", [(j, i) for i, j in down])
-    keep = jnp.stack([here > 0, here < tiles - 1]).astype(jnp.int32)
-    groups = -(-levels * EDGE // width)
-    side = (groups, rows + SUB, width)
-    packed, sent = pl.pallas_call(
-        pack_kernel,
-        in_specs=[vmem()] * 3,
+    from_pair = lax.ppermute(pair_edge, "tiles", swaps(tiles, 0, False))
+    from_step = lax.ppermute(step_edge, "tiles", swaps(tiles, 1, False))
+    own = pl.pallas_call(
+        pack_own_kernel,
+        in_specs=[vmem()],
+        out_specs=vmem(),
+        out_shape=fast((groups, rows, width), F32),
+        name="pack_own",
+    )(held(field))
+    outer, sent = pl.pallas_call(
+        pack_outer_kernel,
+        in_specs=[smem()] + [vmem()] * 3,
         out_specs=[vmem()] * 2,
-        out_shape=[jax.ShapeDtypeStruct(side, F32), jax.ShapeDtypeStruct(side, BF16)],
-        name="pack",
-    )(field, above, below)
-    bands = lax.axis_size("band")
-    east = [(i, (i + 1) % bands) for i in range(bands)]
-    from_west = lax.ppermute(sent, "band", east)
-    from_east = lax.ppermute(sent, "band", [(j, i) for i, j in east])
+        out_shape=[fast((groups, SUB, width), F32), fast((groups, rows + SUB, width), BF16)],
+        name="pack_outer",
+    )(here, held(from_pair), held(from_step), held(own))
+    near = lax.ppermute(sent, "band", swaps(bands, 0, True))
+    far = lax.ppermute(sent, "band", swaps(bands, 1, True))
     inner = pl.pallas_call(
-        main_kernel,
+        functools.partial(main_kernel, tiles),
         in_specs=[smem()] + [vmem()] * 3,
         out_specs=vmem(),
-        out_shape=planes,
+        out_shape=fast(planes, F32),
         name="inner",
-    )(keep, field, above, below)
+    )(here, held(field), held(from_pair), held(from_step))
     smoothed = pl.pallas_call(
-        edge_kernel,
-        in_specs=[smem()] + [vmem()] * 4,
+        functools.partial(edge_kernel, tiles),
+        in_specs=[smem(), smem()] + [vmem()] * 5,
         out_specs=vmem(),
-        out_shape=planes,
-        input_output_aliases={4: 0},
+        out_shape=jax.ShapeDtypeStruct(planes, F32),
         name="edge",
-    )(keep, packed, from_west, from_east, inner)
+    )(here, side, held(own), held(outer), held(near), held(far), held(inner))
     return jnp.swapaxes(heat, 0, 1), jnp.swapaxes(smoothed, 0, 1)
 
 

time: 48.1 us -> 39.6 us (0.82)
  the two profiles are of different devices: /device:TPU:46 before, /device:TPU:40 now
where the time goes in v3:
time: 39.6 us; the launch traced here: 39.4 us
  starting transfers between devices  24.2 us (61%)
  Pallas kernels  11.7 us (30%)
  waiting for transfers between devices  2.77 us (7%)
  between operations  0.71 us (2%)
    ppermute x1, starting transfers between devices, per_device(): from_step = lax.ppermute(step_edge, 'tiles', swaps(tiles, 1, False))  15.5 us
    pallas_call x1, Pallas kernels, per_device(): pl.pallas_call(radiate_kernel, in_specs=[smem(), smem(), smem(), vmem(),...  5.74 us
    ppermute x1, starting transfers between devices, per_device(): far = lax.ppermute(sent, 'band', swaps(bands, 1, True))  4.67 us
    pallas_call x1, Pallas kernels, per_device(): pl.pallas_call(functools.partial(main_kernel, tiles), in_specs=[smem()] +...  3.17 us
    ppermute x1, starting transfers between devices, per_device(): near = lax.ppermute(sent, 'band', swaps(bands, 0, True))  2.13 us
    pallas_call x1, Pallas kernels, per_device(): pl.pallas_call(functools.partial(edge_kernel, tiles), in_specs=[smem(), s...  2.12 us
    ppermute x1, starting transfers between devices, per_device(): from_pair = lax.ppermute(pair_edge, 'tiles', swaps(tiles, 0, False))  1.91 us
    ppermute x1, waiting for transfers between devices, per_device(): from_step = lax.ppermute(step_edge, 'tiles', swaps(tiles, 1, False))  1.84 us
  transfers between devices with their start and end apart: 4, of which 2 were waited for; matrix products, arithmetic and copies ran while one was open for 0% of the time, Pallas kernels for 9%

profile of v3, /device:TPU:40, one launch (start us, length us, event | category | flops | bytes accessed | tf_op | source)
XLA Modules:
  0.0 39.4 jit_solution(18149730479034948987)
XLA Ops:
  0.6 5.7 %radiate.1 = (f32[90,16,128]{2,1,0:T(8,128)}, f32[90,16,128]{2,1,0:T(8,128)S(1)}, bf16[90,4,128]{2,1,0:T(4,128)(2,1)S(1)}, bf16[90,4,128]{2,1,0:T(4,128)(2,1)S(1)}) custom-call(s32[1]{0:T(128)} %bitcast.here_ref, f32[4]{0:T(128)} %weight_ref.1, s32[16]{0:T(128)} %bitcast.10, bf16[16,90,4,128]{3,2,1,0:T(4,128)(2,1)} %depth_ref.1, ...), custom_call_target="tpu_custom_call" | custom-call | tf_op jit(solution)/shard_map/radiate/pallas_call | solution.py:340
  6.4 1.9 %collective-permute-start = (bf16[90,4,128]{2,1,0:T(4,128)(2,1)S(1)}, bf16[90,4,128]{2,1,0:T(4,128)(2,1)S(1)}, u32[]{:S(2)}, u32[]{:S(2)}) collective-permute-start(bf16[90,4,128]{2,1,0:T(4,128)(2,1)S(1)} %get-tuple-element.10), channel_id=1, source_target_pairs={{0,4},{4,0},{8,12},{12,8},{16,20},{20,16},{24,28},{28,24},{32,36},... | collective-permute-start | bytes 276488 | tf_op jit(solution)/shard_map/ppermute | solution.py:354
  8.3 15.5 %collective-permute-start.1 = (bf16[90,4,128]{2,1,0:T(4,128)(2,1)S(1)}, bf16[90,4,128]{2,1,0:T(4,128)(2,1)S(1)}, u32[]{:S(2)}, u32[]{:S(2)}) collective-permute-start(bf16[90,4,128]{2,1,0:T(4,128)(2,1)S(1)} %get-tuple-element.11), channel_id=1, source_target_pairs={{4,8},{8,4},{12,16},{16,12},{20,24},{24,20},{28,32},{32,28},{36,40... | collective-permute-start | bytes 276488 | tf_op jit(solution)/shard_map/ppermute | solution.py:355
  23.8 0.4 pack_own.1.own_ref
  24.1 0.0 collective-permute-done.pair_ref
  24.2 1.8 %collective-permute-done.1.step_ref = bf16[90,4,128]{2,1,0:T(4,128)(2,1)S(1)} collective-permute-done((bf16[90,4,128]{2,1,0:T(4,128)(2,1)S(1)}, bf16[90,4,128]{2,1,0:T(4,128)(2,1)S(1)}, u32[]{:S(2)}, u32[]{:S(2)}) %collective-permute-start.1) | collective-permute-done | bytes 92192 | tf_op jit(solution)/shard_map/ppermute | solution.py:355
  26.0 0.3 pack_outer.1
  26.3 4.7 %collective-permute-start.3 = (bf16[12,24,128]{2,1,0:T(8,128)(2,1)S(1)}, bf16[12,24,128]{2,1,0:T(8,128)(2,1)S(1)}, u32[]{:S(2)}, u32[]{:S(2)}) collective-permute-start(bf16[12,24,128]{2,1,0:T(8,128)(2,1)S(1)} %get-tuple-element.13), channel_id=1, source_target_pairs={{1,2},{2,1},{3,0},{0,3},{5,6},{6,5},{7,4},{4,7},{9,10},{10,9},{11,... | collective-permute-start | bytes 221192 | tf_op jit(solution)/shard_map/ppermute | solution.py:371
  31.0 2.1 %collective-permute-start.2 = (bf16[12,24,128]{2,1,0:T(8,128)(2,1)S(1)}, bf16[12,24,128]{2,1,0:T(8,128)(2,1)S(1)}, u32[]{:S(2)}, u32[]{:S(2)}) collective-permute-start(bf16[12,24,128]{2,1,0:T(8,128)(2,1)S(1)} %get-tuple-element.13), channel_id=1, source_target_pairs={{0,1},{1,0},{2,3},{3,2},{4,5},{5,4},{6,7},{7,6},{8,9},{9,8},{10,11... | collective-permute-start | bytes 221192 | tf_op jit(solution)/shard_map/ppermute | solution.py:370
  33.1 3.2 %inner.1.main_ref = f32[90,16,128]{2,1,0:T(8,128)S(1)} custom-call(s32[1]{0:T(128)} %bitcast.here_ref, f32[90,16,128]{2,1,0:T(8,128)S(1)} %get-tuple-element.9.field_ref, bf16[90,4,128]{2,1,0:T(4,128)(2,1)S(1)} %collective-permute-done.pair_ref, bf16[90,4,128]{2,1,0:T(4,128)(2,1)S(1)} %collective-permute-done.1.step_ref), custom_call_target="tpu_custom_call" | custom-call | tf_op jit(solution)/shard_map/inner/pallas_call | solution.py:372
  36.3 0.0 collective-permute-done.3.far_ref
  36.3 0.9 %collective-permute-done.2.near_ref = bf16[12,24,128]{2,1,0:T(8,128)(2,1)S(1)} collective-permute-done((bf16[12,24,128]{2,1,0:T(8,128)(2,1)S(1)}, bf16[12,24,128]{2,1,0:T(8,128)(2,1)S(1)}, u32[]{:S(2)}, u32[]{:S(2)}) %collective-permute-start.2) | collective-permute-done | bytes 73760 | tf_op jit(solution)/shard_map/ppermute | solution.py:370
  37.3 2.1 %edge.1 = f32[90,16,128]{2,1,0:T(8,128)} custom-call(s32[1]{0:T(128)} %bitcast.here_ref, s32[1]{0:T(128)} %bitcast.5.side_ref, f32[12,16,128]{2,1,0:T(8,128)S(1)} %pack_own.1.own_ref, f32[12,8,128]{2,1,0:T(8,128)S(1)} %get-tuple-element.12.outer_ref, bf16[12,24,128]{2,1,0:T(8,128)(2,1)S(1)} %collective-permute-done.2.near_ref, ...), custom_call_target="tpu_custom_call" | custom-call | tf_op jit(solution)/shard_map/edge/pallas_call | solution.py:379
Async XLA Ops:
  6.4 17.8 %collective-permute-start = (bf16[90,4,128]{2,1,0:T(4,128)(2,1)S(1)}, bf16[90,4,128]{2,1,0:T(4,128)(2,1)S(1)}, u32[]{:S(2)}, u32[]{:S(2)}) collective-permute-start(bf16[90,4,128]{2,1,0:T(4,128)(2,1)S(1)} %get-tuple-element.10), channel_id=1, source_target_pairs={{0,4},{4,0},{8,12},{12,8},{16,20},{20,16},{24,28},{28,24},{32,36},... | collective-permute-start | bytes 276488 | tf_op jit(solution)/shard_map/ppermute | solution.py:354
  8.3 17.7 %collective-permute-start.1 = (bf16[90,4,128]{2,1,0:T(4,128)(2,1)S(1)}, bf16[90,4,128]{2,1,0:T(4,128)(2,1)S(1)}, u32[]{:S(2)}, u32[]{:S(2)}) collective-permute-start(bf16[90,4,128]{2,1,0:T(4,128)(2,1)S(1)} %get-tuple-element.11), channel_id=1, source_target_pairs={{4,8},{8,4},{12,16},{16,12},{20,24},{24,20},{28,32},{32,28},{36,40... | collective-permute-start | bytes 276488 | tf_op jit(solution)/shard_map/ppermute | solution.py:355
  26.3 10.0 %collective-permute-start.3 = (bf16[12,24,128]{2,1,0:T(8,128)(2,1)S(1)}, bf16[12,24,128]{2,1,0:T(8,128)(2,1)S(1)}, u32[]{:S(2)}, u32[]{:S(2)}) collective-permute-start(bf16[12,24,128]{2,1,0:T(8,128)(2,1)S(1)} %get-tuple-element.13), channel_id=1, source_target_pairs={{1,2},{2,1},{3,0},{0,3},{5,6},{6,5},{7,4},{4,7},{9,10},{10,9},{11,... | collective-permute-start | bytes 221192 | tf_op jit(solution)/shard_map/ppermute | solution.py:371
  31.0 6.2 %collective-permute-start.2 = (bf16[12,24,128]{2,1,0:T(8,128)(2,1)S(1)}, bf16[12,24,128]{2,1,0:T(8,128)(2,1)S(1)}, u32[]{:S(2)}, u32[]{:S(2)}) collective-permute-start(bf16[12,24,128]{2,1,0:T(8,128)(2,1)S(1)} %get-tuple-element.13), channel_id=1, source_target_pairs={{0,1},{1,0},{2,3},{3,2},{4,5},{5,4},{6,7},{7,6},{8,9},{9,8},{10,11... | collective-permute-start | bytes 221192 | tf_op jit(solution)/shard_map/ppermute | solution.py:370
